TPU v7x, 256 devices: a whole 4x4x8 slice. The times are simulated.
256 devices in a mesh: wide: 16 (over z, core), ctx: 16 (over y, x).
Axes of the slice: x: 4, y: 4, z: 8, core: 2. Of those that a mesh axis runs over, the one named last changes fastest.
Arguments:
- residual: float32 [256, 4096], P('wide', 'ctx'), may hold values from -40 to 40
- grad_out: float32 [256, 4096], P('wide', 'ctx'), may hold values from -6 to 6
- norm_gain: float32 [4096], P('ctx'), may hold values from 0.5 to 1.5
- w_gate: float32 [4096, 14336], P('ctx', 'wide'), may hold values from -0.09375 to 0.09375
- w_up: float32 [4096, 14336], P('ctx', 'wide'), may hold values from -0.09375 to 0.09375
- w_down: float32 [14336, 4096], P('wide', 'ctx'), may hold values from -0.046875 to 0.046875
- w_out: float32 [4096, 4096], P('wide', 'ctx'), may hold values from -0.09375 to 0.09375
- queries: float32 [256, 4096], P('ctx', 'wide'), may hold values from -12 to 12
- attn_out: float32 [256, 4096], P('ctx', 'wide'), may hold values from -3 to 3
- log_sum_exp: float32 [32, 256], P('wide', 'ctx')
- key_cache: float32 [16, 16384, 128], P('wide', 'ctx'), may hold values from -16 to 16
- value_cache: float32 [16, 16384, 128], P('wide', 'ctx'), may hold values from -6 to 6
Outputs:
- grad_w_gate: float32 [4096, 14336], P('ctx', 'wide')
- grad_w_up: float32 [4096, 14336], P('ctx', 'wide')
- grad_w_down: float32 [14336, 4096], P('wide', 'ctx')
- grad_w_out: float32 [4096, 4096], P('wide', 'ctx')
- grad_resid: float32 [256, 4096], P('wide', 'ctx')
- grad_queries: float32 [256, 4096], P('ctx', 'wide')
All inputs are finite; a program needn't handle non-finite values.
Results may differ from a plain program's by a relative error of at most 0.0003.
Values sent between devices are 32-bit elements; how exact they have to be, the bound alone decides.
A program may use at most 64 MiB of HBM per device.

v0:
```python
import functools
import math

import jax
import jax.numpy as jnp
from jax import lax
from jax.sharding import Mesh
from jax.sharding import PartitionSpec as P

KVH = 8
HD = 128
CTX = ("ctx_0", "ctx_1")


epsilon = 1e-05
highest = lax.Precision.HIGHEST


def swapped(block, axis, bit):
    count = lax.axis_size(axis)
    route = []
    for low in range(count):
        high = low | 1 << bit
        if high != low and high < count:
            route += [(low, high), (high, low)]
    return lax.ppermute(block, axis, route)


def side_by_side(arrays, axis, dim, along):
    ends, at = ([], 0)
    for a in arrays[:-1]:
        at += a.shape[along]
        ends.append(at)
    both = jnp.concatenate(arrays, axis=along)
    return tuple(jnp.split(lax.all_gather(both, axis, axis=dim, tiled=True), ends, axis=along))


def in_blocks(x, dim, length):
    shape = x.shape
    pieces = x.reshape(*shape[:dim], length, shape[dim] // length, *shape[dim + 1 :])
    return jnp.moveaxis(pieces, dim, 0)


def summed_on_arrival(x, axis, dim):
    pieces = in_blocks(x, dim, lax.axis_size(axis))
    arrived = lax.all_to_all(pieces, axis, split_axis=0, concat_axis=0, tiled=True)
    return arrived.sum(axis=0)


def one_axis_at_a_time(x, axes):
    return functools.reduce(lax.psum, axes, x)


def joined_along(pieces, dim):
    pieces = jnp.moveaxis(pieces, 0, dim)
    shape = pieces.shape
    return pieces.reshape(*shape[:dim], shape[dim] * shape[dim + 1], *shape[dim + 2 :])


def copy_for_each(x, axis):
    length = lax.axis_size(axis)
    return lax.all_to_all(jnp.broadcast_to(x[None], (length, *x.shape)), axis, 0, 0, tiled=True)


def collect(x, axis, dim):
    return joined_along(copy_for_each(x, axis), dim)


def rows_first(arrays, axis, dims):
    turned = [jnp.moveaxis(a, dim, 0) for a, dim in zip(arrays, dims)]
    widths = [t[0].size for t in turned]
    both = jnp.concatenate([t.reshape(-1, w) for t, w in zip(turned, widths)], axis=1)
    filled = lax.all_gather(both, axis, axis=0, tiled=True)
    pieces = jnp.split(filled, [sum(widths[:k]) for k in range(1, len(widths))], axis=1)
    return tuple(
        (
            jnp.moveaxis(b.reshape(-1, *t.shape[1:]), 0, dim)
            for b, t, dim in zip(pieces, turned, dims)
        )
    )


def matmul(left, right):
    return jnp.dot(left, right, precision=highest, preferred_element_type=jnp.float32)


def matmul_tn(left, right):
    return lax.dot_general(
        left, right, (((0,), (0,)), ((), ())), precision=highest, preferred_element_type=jnp.float32
    )


def matmul_nt(left, right):
    return lax.dot_general(
        left, right, (((1,), (1,)), ((), ())), precision=highest, preferred_element_type=jnp.float32
    )


def join_group(own_part, far_part, upper):
    joined = []
    for own_item, far_item, join_dim in zip(own_part, far_part, (1, 1, 0, 0)):
        lower_first = jnp.concatenate((own_item, far_item), axis=join_dim)
        upper_first = jnp.concatenate((far_item, own_item), axis=join_dim)
        joined.append(jnp.where(upper, upper_first, lower_first))
    return tuple(joined)


def halve_group(partial_sums, member, split):
    for bit_index in reversed(range(split.bit_length() - 1)):
        half_width = partial_sums.shape[1] // 2
        upper = member // (1 << bit_index) % 2 == 1
        lower_half = partial_sums[:, :half_width]
        upper_half = partial_sums[:, half_width:]
        kept_half = jnp.where(upper, upper_half, lower_half)
        sent_half = jnp.where(upper, lower_half, upper_half)
        partial_sums = kept_half + swapped(sent_half, "wide", bit_index)
    return partial_sums


def shards(
    residual,
    grad_out,
    norm_gain,
    w_gate,
    w_up,
    w_down,
    w_out,
    queries,
    attn_out,
    log_sum_exp,
    key_cache,
    value_cache,
):
    width = residual.shape[1] * lax.axis_size(CTX)
    all_resid, all_grad = side_by_side((residual, grad_out), "wide", 0, 1)
    gained = all_resid * norm_gain[None, :]
    gate_raw, up_raw, d_hidden, squares = lax.psum(
        (
            matmul(gained, w_gate),
            matmul(gained, w_up),
            matmul_nt(all_grad, w_down),
            jnp.sum(all_resid * all_resid, axis=1),
        ),
        CTX,
    )
    inv_rms = lax.rsqrt(squares / width + epsilon)
    normed = gained * inv_rms[:, None]
    gate_out = gate_raw * inv_rms[:, None]
    up_out = up_raw * inv_rms[:, None]
    sigmoid_gate = jax.nn.sigmoid(gate_out)
    activated = gate_out * sigmoid_gate
    hidden = activated * up_out
    grad_w_down = matmul_tn(hidden, all_grad)
    d_up = d_hidden * activated
    d_gate = d_hidden * up_out * sigmoid_gate * (1.0 + gate_out * (1.0 - sigmoid_gate))
    grad_w_gate = matmul_tn(normed, d_gate)
    grad_w_up = matmul_tn(normed, d_up)
    own_rows = residual.shape[0]
    d_normed = summed_on_arrival(matmul_nt(d_gate, w_gate) + matmul_nt(d_up, w_up), "wide", 0)
    scaled = d_normed * norm_gain[None, :]
    row_dot = one_axis_at_a_time(jnp.sum(residual * scaled, axis=1), CTX)
    own_inv = lax.dynamic_slice_in_dim(inv_rms, lax.axis_index("wide") * own_rows, own_rows, 0)
    cubed = own_inv * own_inv * own_inv
    grad_resid = (
        grad_out + own_inv[:, None] * scaled - residual * (cubed * row_dot / width)[:, None]
    )
    gathered_resid = collect(grad_resid, "wide", 0)
    d_attn = summed_on_arrival(matmul_nt(gathered_resid, w_out), CTX, 0)
    all_queries, all_outputs, all_dattn, all_lse = rows_first(
        (queries, attn_out, d_attn, log_sum_exp), CTX, (0, 0, 0, 1)
    )
    grad_w_out = matmul_tn(all_outputs, gathered_resid)
    rows_total = all_queries.shape[0]
    head_dim = HD
    local_heads = all_queries.shape[1] // head_dim
    delta = jnp.sum((all_dattn * all_outputs).reshape(rows_total, local_heads, head_dim), axis=2).T
    split = lax.axis_size("wide") // KVH
    member = lax.axis_index("wide") % split
    group = (all_queries, all_dattn, all_lse, delta)
    partner = swapped(group, "wide", 0)
    upper = member // (1 << 0) % 2 == 1
    group = join_group(group, partner, upper)
    group_queries, group_dattn, group_lse, group_delta = group
    group_count = group_queries.shape[1] // head_dim
    query_rows = (
        group_queries.reshape(rows_total, group_count, head_dim)
        .transpose(1, 0, 2)
        .reshape(group_count * rows_total, head_dim)
    )
    dout_rows = (
        group_dattn.reshape(rows_total, group_count, head_dim)
        .transpose(1, 0, 2)
        .reshape(group_count * rows_total, head_dim)
    )
    lse_rows = group_lse.reshape(group_count * rows_total)
    delta_rows = group_delta.reshape(group_count * rows_total)
    keys_local = key_cache[0]
    values_local = value_cache[0]
    key_count = keys_local.shape[0]
    ctx_count = lax.axis_size(CTX)
    context = key_count * ctx_count * split
    key_base = member * (key_count * ctx_count) + lax.axis_index(CTX) * key_count
    query_pos = jnp.tile(jnp.arange(rows_total, dtype=jnp.int32), group_count) + (
        context - rows_total
    )
    scale = 1.0 / math.sqrt(head_dim)
    block = min(512, key_count)
    accum = jnp.zeros((group_count * rows_total, head_dim), jnp.float32)
    for block_index in range(key_count // block):
        key_block = keys_local[block_index * block : (block_index + 1) * block]
        value_block = values_local[block_index * block : (block_index + 1) * block]
        key_pos = key_base + block_index * block + jnp.arange(block, dtype=jnp.int32)
        scores = matmul_nt(query_rows, key_block) * scale
        probs = jnp.where(
            key_pos[None, :] <= query_pos[:, None], jnp.exp(scores - lse_rows[:, None]), 0.0
        )
        dprobs = matmul_nt(dout_rows, value_block)
        accum = accum + matmul(probs * (dprobs - delta_rows[:, None]), key_block)
    dq_group = (
        (accum * scale)
        .reshape(group_count, rows_total, head_dim)
        .transpose(1, 0, 2)
        .reshape(rows_total, group_count * head_dim)
    )
    halved = halve_group(dq_group, member, split)
    grad_queries = summed_on_arrival(halved, CTX, 0)
    return (grad_w_gate, grad_w_up, grad_w_down, grad_w_out, grad_resid, grad_queries)


def solution(mesh):
    torus = Mesh(mesh.devices.reshape(mesh.shape["wide"], 4, 4), ("wide", "ctx_0", "ctx_1"))
    return jax.shard_map(
        shards,
        mesh=torus,
        in_specs=(
            P("wide", CTX),
            P("wide", CTX),
            P(CTX),
            P(CTX, "wide"),
            P(CTX, "wide"),
            P("wide", CTX),
            P("wide", CTX),
            P(CTX, "wide"),
            P(CTX, "wide"),
            P("wide", CTX),
            P("wide", CTX, None),
            P("wide", CTX, None),
        ),
        out_specs=(
            P(CTX, "wide"),
            P(CTX, "wide"),
            P("wide", CTX),
            P("wide", CTX),
            P("wide", CTX),
            P(CTX, "wide"),
        ),
        check_vma=False,
    )
```

profile of v0, /device:TPU:1, one launch (start us, length us, event | category | flops | bytes accessed | tf_op | source)
XLA Modules:
  0.0 293.4 jit_solution(3167440317429720697)
XLA Ops:
  7.2 0.8 pad_maximum_fusion.1
  8.0 22.7 %all_gather.6 = f32[256,512]{1,0:T(8,128)S(1)} all-gather(f32[16,512]{1,0:T(8,128)S(1)} %pad_maximum_fusion.1), channel_id=1, replica_groups=mesh['wide'=16,'ctx_0'=4,'ctx_1'=4] {'wide'}, dimensions={0}, use_global_device_ids=true | all-gather | bytes 557056 | tf_op jit(solution)/shard_map/all_gather | solution.py:35
  30.8 3.2 %fusion.59 = f32[256,896]{1,0:T(8,128)} fusion(f32[896,256]{1,0:T(8,128)} %param.17, f32[256,512]{1,0:T(8,128)S(1)} %all_gather.6), kind=kOutput, calls=%fused_computation.64 | convolution fusion | flops 704643072 | bytes 2097152 | tf_op jit(solution)/shard_map/dot_general | solution.py:94
  34.0 2.0 fusion.68
  35.9 2.0 fusion.69
  38.0 33.9 %psum.42 = f32[256]{0:T(256)S(1)} all-reduce(f32[256]{0:T(256)S(1)} %multiply_reduce_fusion), channel_id=1, replica_groups=mesh['wide'=16,'ctx_0'=4,'ctx_1'=4] {'ctx_0','ctx_1'}, use_global_device_ids=true, to_apply=%region_1.0 | all-reduce | flops 256 | bytes 2048 | tf_op jit(solution)/shard_map/psum | solution.py:137
  71.9 67.0 %all-reduce.3.cloned.1.call-done = (f32[256,896]{1,0:T(8,128)}, f32[256,896]{1,0:T(8,128)}, f32[256,896]{1,0:T(8,128)}) async-done(((f32[256,896]{1,0:T(8,128)}, f32[256,896]{1,0:T(8,128)}, f32[256,896]{1,0:T(8,128)}), (f32[256,896]{1,0:T(8,128)}, f32[256,896]{1,0:T(8,128)}, f32[256,896]{1,0:T(8,128)})) %all-reduce.3.cloned.1.call-update) | async-done | bytes 2752528 | tf_op jit(solution)/shard_map/psum | solution.py:137
  138.9 2.3 add_multiply_fusion
  141.2 1.0 fusion.90
  142.3 1.9 convolution_add_fusion
  144.2 8.7 %all-to-all-start = ((f32[16,16,256]{2,1,0:T(8,128)}), f32[16,16,256]{2,1,0:T(8,128)S(1)}, u32[]{:S(2)}, u32[]{:S(2)}) async-start(f32[16,16,256]{2,1,0:T(8,128)} %bitcast), calls=%async_computation | async-start | bytes 524288 | tf_op jit(solution)/shard_map/all_to_all | solution.py:46
  152.9 11.6 %all-to-all-done = f32[16,16,256]{2,1,0:T(8,128)S(1)} async-done(((f32[16,16,256]{2,1,0:T(8,128)}), f32[16,16,256]{2,1,0:T(8,128)S(1)}, u32[]{:S(2)}, u32[]{:S(2)}) %all-to-all-start) | async-done | bytes 262176 | tf_op jit(solution)/shard_map/all_to_all | solution.py:46
  164.7 7.7 %psum.46 = f32[16]{0:T(128)S(1)} all-reduce(f32[16]{0:T(128)S(1)} %multiply_reduce_fusion.1), channel_id=1, replica_groups=mesh['wide'=16,'ctx_0'=4,'ctx_1'=4] {'ctx_0'}, use_global_device_ids=true, to_apply=%region_7.0 | all-reduce | flops 16 | bytes 128 | tf_op jit(solution)/shard_map/psum | solution.py:51
  172.4 7.4 %psum.47 = f32[16]{0:T(128)S(1)} all-reduce(f32[16]{0:T(128)S(1)} %psum.46), channel_id=1, replica_groups=mesh['wide'=16,'ctx_0'=4,'ctx_1'=4] {'ctx_1'}, use_global_device_ids=true, to_apply=%region_8.0 | all-reduce | flops 16 | bytes 128 | tf_op jit(solution)/shard_map/psum | solution.py:51
  180.0 18.1 %all_to_all.20 = f32[16,16,256]{2,1,0:T(8,128)S(1)} all-to-all(f32[16,16,256]{2,1,0:T(8,128)S(1)} %broadcast_in_dim.6), channel_id=1, replica_groups=mesh['wide'=16,'ctx_0'=4,'ctx_1'=4] {'wide'}, dimensions={0} | all-to-all | bytes 524288 | tf_op jit(solution)/shard_map/all_to_all | solution.py:62
  198.0 0.7 copy-done.7
  198.8 1.1 fusion.54
  199.9 3.5 %all-to-all-start.2 = ((f32[16,16,256]{2,1,0:T(8,128)}), f32[16,16,256]{2,1,0:T(8,128)S(1)}, u32[]{:S(2)}, u32[]{:S(2)}) async-start(f32[16,16,256]{2,1,0:T(8,128)} %fusion.54), calls=%async_computation.2 | async-start | bytes 524288 | tf_op jit(solution)/shard_map/all_to_all | solution.py:46
  203.5 0.6 copy.54
  204.1 0.6 iota_add_fusion.1
  204.7 0.6 iota_add_fusion
  205.3 7.2 %all-to-all-done.2 = f32[16,16,256]{2,1,0:T(8,128)S(1)} async-done(((f32[16,16,256]{2,1,0:T(8,128)}), f32[16,16,256]{2,1,0:T(8,128)S(1)}, u32[]{:S(2)}, u32[]{:S(2)}) %all-to-all-start.2) | async-done | bytes 262176 | tf_op jit(solution)/shard_map/all_to_all | solution.py:46
  212.6 17.2 %all_gather.7 = f32[256,770]{1,0:T(8,128)S(1)} all-gather(f32[16,770]{1,0:T(8,128)S(1)} %pad_maximum_fusion), channel_id=1, replica_groups=mesh['wide'=16,'ctx_0'=4,'ctx_1'=4] {'ctx_0','ctx_1'}, dimensions={0}, use_global_device_ids=true | all-gather | bytes 837760 | tf_op jit(solution)/shard_map/all_gather | solution.py:73
  230.0 5.9 %collective-permute-start.2 = (f32[256,256]{0,1:T(8,128)S(1)}, f32[256,256]{0,1:T(8,128)}, u32[]{:S(2)}, u32[]{:S(2)}) collective-permute-start(f32[256,256]{0,1:T(8,128)S(1)} %copy.53), channel_id=1, source_target_pairs={{0,16},{16,0},{32,48},{48,32},{64,80},{80,64},{96,112},{112,96},{1... | collective-permute-start | bytes 786440 | tf_op jit(solution)/shard_map/ppermute | solution.py:26
  236.2 0.5 collective-permute-start.3
  236.7 3.7 %fusion.42 = f32[256,896]{1,0:T(8,128)} fusion(f32[256,896]{1,0:T(8,128)} %get-tuple-element.6, f32[256,512]{1,0:T(8,128)S(1)} %all_gather.6, f32[256]{0:T(256)} %copy-done.23, f32[256]{0:T(256)} %param.14, f32[256,896]{1,0:T(8,128)} %get-tuple-element.7), kind=kOutput, calls=%fused_computation.43 | convolution fusion | flops 706150400 | bytes 3017728 | tf_op jit(solution)/shard_map/dot_general | solution.py:88
  240.5 0.8 copy.52
  241.4 1.0 copy.43
  242.5 1.1 fusion.39
  243.6 0.2 copy.48
  243.8 0.8 copy-done.5
  244.6 4.1 %fusion.44 = f32[1024,512]{1,0:T(8,128)} fusion(f32[1024,128]{1,0:T(8,128)S(1)} %bitcast.66, f32[1,1024,128]{2,1,0:T(8,128)} %param.23), kind=kOutput, calls=%fused_computation.45 | convolution fusion | flops 805306368 | bytes 2883584 | tf_op jit(solution)/shard_map/dot_general | solution.py:94
  248.6 2.8 fusion.49
  251.5 2.1 fusion.38
  253.6 2.0 copy.42
  255.6 3.0 %fusion.47 = f32[1024,512]{1,0:T(8,128)S(1)} fusion(f32[1024,128]{1,0:T(8,128)} %bitcast.68, f32[1,1024,128]{2,1,0:T(8,128)} %param.22), kind=kOutput, calls=%fused_computation.48 | convolution fusion | flops 805306368 | bytes 2883584 | tf_op jit(solution)/shard_map/dot_general | solution.py:94
  258.7 1.8 fusion.52
  260.5 2.2 fusion
  262.8 3.3 %fusion.19 = f32[1024,128]{1,0:T(8,128)} fusion(f32[1024,128]{1,0:T(8,128)S(1)} %fusion, f32[1024,512]{1,0:T(8,128)S(1)} %fusion.49, f32[1024,512]{1,0:T(8,128)S(1)} %fusion.52, f32[1024]{0:T(1024)S(1)} %bitcast.76, f32[1024]{0:T(1024)S(1)} %bitcast.78, s32[512]{0:T(512)S(1)} %copy-done.25, s32[1024]{0:T(1024)S(1)} %bitcast.74, ...), kind=kOutput, calls=%fused_computation.17 | convolution fusion | flops 808714240 | bytes 5519360 | tf_op jit(solution)/shard_map/dot_general | solution.py:84
  266.1 1.2 copy.49
  267.4 0.7 collective-permute-start.4
  268.1 4.2 %fusion.34 = f32[896,256]{1,0:T(8,128)} fusion(f32[256,896]{1,0:T(8,128)} %get-tuple-element.8, f32[256]{0:T(256)S(1)} %copy-done.24, f32[256,512]{1,0:T(8,128)S(1)} %all_gather.6, f32[256,896]{1,0:T(8,128)} %get-tuple-element.7), kind=kOutput, calls=%fused_computation.31 | convolution fusion | flops 706248704 | bytes 3015680 | tf_op jit(solution)/shard_map/dot_general | solution.py:88
  272.4 0.8 copy.50
  273.2 4.3 %all-to-all-start.3 = ((f32[16,16,256]{2,1,0:T(8,128)}), f32[16,16,256]{2,1,0:T(8,128)S(1)}, u32[]{:S(2)}, u32[]{:S(2)}) async-start(f32[16,16,256]{2,1,0:T(8,128)} %bitcast.23), calls=%async_computation.3 | async-start | bytes 524288 | tf_op jit(solution)/shard_map/all_to_all | solution.py:46
  277.5 2.0 fusion.66
  279.5 2.2 fusion.84
  281.8 4.1 %all-to-all-done.3 = f32[16,16,256]{2,1,0:T(8,128)S(1)} async-done(((f32[16,16,256]{2,1,0:T(8,128)}), f32[16,16,256]{2,1,0:T(8,128)S(1)}, u32[]{:S(2)}, u32[]{:S(2)}) %all-to-all-start.3) | async-done | bytes 262176 | tf_op jit(solution)/shard_map/all_to_all | solution.py:46
  285.9 0.6 reduce_sum.59
  (85 shorter events, 1.5 us)
Async XLA Ops:
  7.2 26.8 %copy-start = (f32[256,896]{1,0:T(8,128)S(1)}, f32[256,896]{1,0:T(8,128)}, u32[]{:S(2)}) copy-start(f32[256,896]{1,0:T(8,128)} %param.15) | copy-start | bytes 2752516
  7.2 26.8 %copy-start.19 = (f32[256]{0:T(256)S(1)}, f32[256]{0:T(256)}, u32[]{:S(2)}) copy-start(f32[256]{0:T(256)} %param.14) | copy-start | bytes 3076
  7.2 131.7 %all-reduce.3.cloned.1.call-start = ((), (), s32[]{:S(2)}) async-start(), calls=%async_computation.4 | async-start | bytes 5505024 | tf_op jit(solution)/shard_map/psum | solution.py:137
  30.8 5.2 %copy-start.10 = (f32[256,896]{1,0:T(8,128)S(1)}, f32[256,896]{1,0:T(8,128)}, u32[]{:S(2)}) copy-start(f32[256,896]{1,0:T(8,128)} %param.16) | copy-start | bytes 2752516
  71.9 107.8 %copy-start.23 = (f32[256]{0:T(256)}, f32[256]{0:T(256)S(1)}, u32[]{:S(2)}) copy-start(f32[256]{0:T(256)S(1)} %add_rsqrt_fusion) | copy-start | bytes 3076
  138.9 3.4 %copy-start.11 = (f32[256,896]{1,0:T(8,128)S(1)}, f32[256,896]{1,0:T(8,128)}, u32[]{:S(2)}) copy-start(f32[256,896]{1,0:T(8,128)} %get-tuple-element.7) | copy-start | bytes 2752516
  138.9 3.4 %copy-start.12 = (f32[256,896]{1,0:T(8,128)S(1)}, f32[256,896]{1,0:T(8,128)}, u32[]{:S(2)}) copy-start(f32[256,896]{1,0:T(8,128)} %get-tuple-element.6) | copy-start | bytes 2752516
  141.2 3.0 %copy-start.2 = (f32[256,896]{1,0:T(8,128)}, f32[256,896]{1,0:T(8,128)S(1)}, u32[]{:S(2)}) copy-start(f32[256,896]{1,0:T(8,128)S(1)} %add_multiply_fusion) | copy-start | bytes 2752516
  142.3 22.3 %copy-start.15 = (f32[16,256]{1,0:T(8,128)S(1)}, f32[16,256]{1,0:T(8,128)}, u32[]{:S(2)}) copy-start(f32[16,256]{1,0:T(8,128)} %param.12) | copy-start | bytes 49156
  142.3 37.6 %copy-start.17 = (f32[16,256]{1,0:T(8,128)S(1)}, f32[16,256]{1,0:T(8,128)}, u32[]{:S(2)}) copy-start(f32[16,256]{1,0:T(8,128)} %param.13) | copy-start | bytes 49156
  142.3 56.5 %copy-start.14 = (f32[256,256]{1,0:T(8,128)S(1)}, f32[256,256]{1,0:T(8,128)}, u32[]{:S(2)}) copy-start(f32[256,256]{1,0:T(8,128)} %param.18) | copy-start | bytes 786436
  144.2 59.2 %copy-start.27 = (f32[2,16]{1,0:T(2,128)S(1)}, f32[2,16]{1,0:T(2,128)}, u32[]{:S(2)}) copy-start(f32[2,16]{1,0:T(2,128)} %param.21) | copy-start | bytes 388
  144.2 68.3 %copy-start.21 = (f32[16,256]{1,0:T(8,128)S(1)}, f32[16,256]{1,0:T(8,128)}, u32[]{:S(2)}) copy-start(f32[16,256]{1,0:T(8,128)} %param.20) | copy-start | bytes 49156
  144.2 68.3 %copy-start.22 = (f32[16,256]{1,0:T(8,128)S(1)}, f32[16,256]{1,0:T(8,128)}, u32[]{:S(2)}) copy-start(f32[16,256]{1,0:T(8,128)} %param.19) | copy-start | bytes 49156
  144.2 20.3 %all-to-all-start = ((f32[16,16,256]{2,1,0:T(8,128)}), f32[16,16,256]{2,1,0:T(8,128)S(1)}, u32[]{:S(2)}, u32[]{:S(2)}) async-start(f32[16,16,256]{2,1,0:T(8,128)} %bitcast), calls=%async_computation | async-start | bytes 524288 | tf_op jit(solution)/shard_map/all_to_all | solution.py:46
  179.9 49.9 %copy-start.16 = (f32[16,256]{1,0:T(8,128)}, f32[16,256]{1,0:T(8,128)S(1)}, u32[]{:S(2)}) copy-start(f32[16,256]{1,0:T(8,128)S(1)} %multiply_subtract_fusion) | copy-start | bytes 49156
  198.0 0.7 copy-start.7
  199.9 12.6 %all-to-all-start.2 = ((f32[16,16,256]{2,1,0:T(8,128)}), f32[16,16,256]{2,1,0:T(8,128)S(1)}, u32[]{:S(2)}, u32[]{:S(2)}) async-start(f32[16,16,256]{2,1,0:T(8,128)} %fusion.54), calls=%async_computation.2 | async-start | bytes 524288 | tf_op jit(solution)/shard_map/all_to_all | solution.py:46
  229.7 10.7 %copy-start.4 = (f32[256,770]{1,0:T(8,128)}, f32[256,770]{1,0:T(8,128)S(1)}, u32[]{:S(2)}) copy-start(f32[256,770]{1,0:T(8,128)S(1)} %all_gather.7) | copy-start | bytes 2365444
  230.0 12.5 %collective-permute-start.2 = (f32[256,256]{0,1:T(8,128)S(1)}, f32[256,256]{0,1:T(8,128)}, u32[]{:S(2)}, u32[]{:S(2)}) collective-permute-start(f32[256,256]{0,1:T(8,128)S(1)} %copy.53), channel_id=1, source_target_pairs={{0,16},{16,0},{32,48},{48,32},{64,80},{80,64},{96,112},{112,96},{1... | collective-permute-start | bytes 786440 | tf_op jit(solution)/shard_map/ppermute | solution.py:26
  235.9 5.5 %collective-permute-start.1 = (f32[2,256]{0,1:T(8,128)S(1)}, f32[2,256]{0,1:T(8,128)}, u32[]{:S(2)}, u32[]{:S(2)}) collective-permute-start(f32[2,256]{0,1:T(8,128)S(1)} %slice_bitcast_fusion), channel_id=1, source_target_pairs={{0,16},{16,0},{32,48},{48,32},{64,80},{80,64},{96,112},{112,96},{1... | collective-permute-start | bytes 6152 | tf_op jit(solution)/shard_map/ppermute | solution.py:26
  236.2 6.2 %collective-permute-start.3 = (f32[2,256]{1,0:T(2,128)S(1)}, f32[2,256]{1,0:T(2,128)S(1)}, u32[]{:S(2)}, u32[]{:S(2)}) collective-permute-start(f32[2,256]{1,0:T(2,128)S(1)} %bitcast.80), channel_id=1, source_target_pairs={{0,16},{16,0},{32,48},{48,32},{64,80},{80,64},{96,112},{112,96},{1... | collective-permute-start | bytes 6152 | tf_op jit(solution)/shard_map/ppermute | solution.py:26
  241.3 10.2 %collective-permute-start = (f32[256,256]{0,1:T(8,128)}, f32[256,256]{0,1:T(8,128)}, u32[]{:S(2)}, u32[]{:S(2)}) collective-permute-start(f32[256,256]{0,1:T(8,128)} %copy.52), channel_id=1, source_target_pairs={{0,16},{16,0},{32,48},{48,32},{64,80},{80,64},{96,112},{112,96},{1... | collective-permute-start | bytes 786440 | tf_op jit(solution)/shard_map/ppermute | solution.py:26
  243.8 0.8 copy-start.5
  243.8 4.9 %copy-start.13 = (f32[1,1024,128]{2,1,0:T(8,128)S(1)}, f32[1,1024,128]{2,1,0:T(8,128)}, u32[]{:S(2)}) copy-start(f32[1,1024,128]{2,1,0:T(8,128)} %param.23) | copy-start | bytes 1572868
  255.6 3.0 %copy-start.6 = (f32[4,256,128]{2,1,0:T(8,128)S(1)}, f32[4,256,128]{2,1,0:T(8,128)}, u32[]{:S(2)}) copy-start(f32[4,256,128]{2,1,0:T(8,128)} %copy.42) | copy-start | bytes 1572868
  255.6 3.0 %copy-start.9 = (f32[1,1024,128]{2,1,0:T(8,128)S(1)}, f32[1,1024,128]{2,1,0:T(8,128)}, u32[]{:S(2)}) copy-start(f32[1,1024,128]{2,1,0:T(8,128)} %param.22) | copy-start | bytes 1572868
  258.6 1.8 copy-start.1
  258.6 1.8 copy-start.18
  258.7 1.8 copy-start.26
  260.5 2.2 copy-start.25
  262.8 5.3 %copy-start.24 = (f32[256]{0:T(256)S(1)}, f32[256]{0:T(256)}, u32[]{:S(2)}) copy-start(f32[256]{0:T(256)} %copy-done.23) | copy-start | bytes 3076
  267.4 4.9 %collective-permute-start.4 = (f32[256,256]{0,1:T(8,128)S(1)}, f32[256,256]{0,1:T(8,128)S(1)}, u32[]{:S(2)}, u32[]{:S(2)}) collective-permute-start(f32[256,256]{0,1:T(8,128)S(1)} %slice_select_fusion), channel_id=1, source_target_pairs={{0,16},{16,0},{32,48},{48,32},{64,80},{80,64},{96,112},{112,96},{1... | collective-permute-start | bytes 786440 | tf_op jit(solution)/shard_map/ppermute | solution.py:26
  272.3 5.2 %copy-start.3 = (f32[256,896]{1,0:T(8,128)S(1)}, f32[256,896]{1,0:T(8,128)}, u32[]{:S(2)}) copy-start(f32[256,896]{1,0:T(8,128)} %copy-done.2) | copy-start | bytes 2752516
  272.3 5.2 %copy-start.20 = (f32[256]{0:T(256)S(1)}, f32[256]{0:T(256)}, u32[]{:S(2)}) copy-start(f32[256]{0:T(256)} %param.14) | copy-start | bytes 3076
  272.3 7.2 %copy-start.8 = (f32[16,16,256]{2,1,0:T(8,128)S(1)}, f32[16,16,256]{2,1,0:T(8,128)}, u32[]{:S(2)}) copy-start(f32[16,16,256]{2,1,0:T(8,128)} %copy-done.7) | copy-start | bytes 786436
  273.2 12.7 %all-to-all-start.3 = ((f32[16,16,256]{2,1,0:T(8,128)}), f32[16,16,256]{2,1,0:T(8,128)S(1)}, u32[]{:S(2)}, u32[]{:S(2)}) async-start(f32[16,16,256]{2,1,0:T(8,128)} %bitcast.23), calls=%async_computation.3 | async-start | bytes 524288 | tf_op jit(solution)/shard_map/all_to_all | solution.py:46
Sparse Core Ops, SparseCore 0:
  38.0 100.8 all-reduce.2
where the time goes:
time: 294 us; the launch traced here: 293 us
  blocking collectives  107 us (36%)
  waiting for transfers between devices  89.9 us (31%)
  matrix products  40.7 us (14%)
  starting transfers between devices  23.9 us (8%)
  between operations  14.5 us (5%)
  local copies, waits for them, and re-layouts  8.82 us (3%)
  other arithmetic  8.64 us (3%)
    psum x1, waiting for transfers between devices, shards(): lax.psum((matmul(gained, w_gate), matmul(gained, w_up), matmul_nt(all_gra...  67 us
    psum x1, blocking collectives, shards(): lax.psum((matmul(gained, w_gate), matmul(gained, w_up), matmul_nt(all_gra...  33.9 us
    all_to_all x3, waiting for transfers between devices, summed_on_arrival(): lax.all_to_all(pieces, axis, split_axis=0, concat_axis=0, tiled=True)  22.9 us
    all_gather x1, blocking collectives, side_by_side(): lax.all_gather(both, axis, axis=dim, tiled=True)  22.7 us
    dot_general x8, matrix products, matmul_nt(): lax.dot_general(left, right, (((1,), (1,)), ((), ())), precision=highest,...  19 us
    all_to_all x1, blocking collectives, copy_for_each(): lax.all_to_all(jnp.broadcast_to(x[None], (length, *x.shape)), axis, 0, 0,...  18.1 us
    all_gather x1, blocking collectives, rows_first(): filled = lax.all_gather(both, axis, axis=0, tiled=True)  17.2 us
    all_to_all x3, starting transfers between devices, summed_on_arrival(): lax.all_to_all(pieces, axis, split_axis=0, concat_axis=0, tiled=True)  16.5 us
  transfers between devices with their start and end apart: 9, of which 4 were waited for; matrix products, arithmetic and copies ran while one was open for 8% of the time, Pallas kernels for 0%

commit v1 on v0

v1 whole, which is shorter than its diff:
```python
import math

import jax
import jax.numpy as jnp
from jax import lax
from jax.experimental import pallas as pl
from jax.experimental.pallas import tpu as pltpu
from jax.sharding import Mesh
from jax.sharding import PartitionSpec as P

MESH = pl.DeviceIdType.MESH
F32 = jnp.float32
BF16 = jnp.bfloat16
EPS = 1e-05
NZ, NX, NY = 8, 4, 4
NCTX = NX * NY
OFF = (0, 1, -1, 2, -2, 3, -3, 4)
SLOT = {o: s for s, o in enumerate(OFF)}
D, FF, HD = 4096, 14336, 128
WD, WF = D // NCTX, FF // 16
ROWS, BR = 256, 16
HALF = 11 * 128
WIDTH = 2 * HALF
KEYS = 1024
CONTEXT = 32768
SCALE = 1.0 / math.sqrt(HD)


def split(v):
    hi = v.astype(BF16)
    return hi, (v - hi.astype(F32)).astype(BF16)


def nn(a, b):
    return lax.dot_general(a, b, (((1,), (0,)), ((), ())), preferred_element_type=F32)


def nt(a, b):
    return lax.dot_general(a, b, (((1,), (1,)), ((), ())), preferred_element_type=F32)


def three(a, bh, bl, dot):
    ah, al = split(a)
    m = a.shape[0]
    both = dot(jnp.concatenate([ah, al], axis=0), bh)
    return both[:m] + both[m:] + dot(ah, bl)


def kernel(
    resid_h, grad_h, gain_h, wg_h, wu_h, wd_h, wo_h, qol_h, key_h, val_h,
    gwg_o, gwu_o, gwd_o, gwo_o, gres_o, gq_o,
    rg, gain, w2f, wdf, wof, w2h, w2l, wdh, wdl, woh, wol, qol, kv, k3, v3,
    part, r1, d1, c1, q1, r2, d2, c2, full, tpart, tpair, usum, rz, gres, da, rda, dat,
    probs, acc, dq, rdq, gw2, gwd, gwo, gqs,
    lsem, ssem, rsem,
):
    z, core = lax.axis_index("z"), lax.axis_index("core")
    y, x = lax.axis_index("y"), lax.axis_index("x")
    me = y * NX + x
    other = 1 - core
    wide = 2 * z + core

    counter = {"l": 0, "r": 0}
    started = []

    def local(src, dst):
        copy = pltpu.make_async_copy(src, dst, lsem.at[counter["l"]])
        counter["l"] += 1
        copy.start()
        return copy

    def send(src, dst, dev):
        n = counter["r"]
        counter["r"] += 1
        copy = pltpu.make_async_remote_copy(
            src_ref=src, dst_ref=dst, send_sem=ssem.at[n], recv_sem=rsem.at[n],
            device_id=dev, device_id_type=MESH,
        )
        copy.start()
        started.append(copy)
        return copy

    def at_z(o):
        return {"z": lax.rem(z + (o + NZ), NZ)}

    def at_x(o):
        return {"x": lax.rem(x + (o + NX), NX)}

    def at_y(o):
        return {"y": lax.rem(y + (o + NY), NY)}

    pair = {"core": other}
    ctx_offsets = sorted(
        [(dy, dx) for dy in range(NY) for dx in range(NX) if (dy, dx) != (0, 0)],
        key=lambda o: -(min(o[0], 4 - o[0]) + min(o[1], 4 - o[1])),
    )

    def at_ctx(dy, dx):
        return {"y": lax.rem(y + dy, NY), "x": lax.rem(x + dx, NX)}

    def ctx_of(dy, dx):
        return lax.rem(y + dy, NY) * NX + lax.rem(x + dx, NX)

    l_rg = [local(resid_h, rg.at[0, core, 0]), local(grad_h, rg.at[0, core, 1])]
    l_qol = local(qol_h, qol.at[me])
    l_gain = local(gain_h, gain)
    l_w = [local(wg_h, w2f.at[0]), local(wu_h, w2f.at[1]), local(wd_h, wdf), local(wo_h, wof)]
    l_kv = [local(key_h.at[0], kv.at[0, core]), local(val_h.at[0], kv.at[1, core])]

    barrier = pltpu.get_barrier_semaphore()
    peers = [pair] + [at_z(o) for o in OFF[1:]] + [at_ctx(*o) for o in ctx_offsets]
    for dev in peers:
        pl.semaphore_signal(barrier, inc=1, device_id=dev, device_id_type=MESH)
    pl.semaphore_wait(barrier, len(peers))

    for c in l_rg:
        c.wait()
    zp, zm, pr = {}, {}, {}

    def zsend(bag, o, s_from, s_to, sub=None):
        a = rg.at[s_from, core] if sub is None else rg.at[s_from, core, sub]
        b = rg.at[s_to, core] if sub is None else rg.at[s_to, core, sub]
        bag[s_to] = send(a, b, at_z(o))

    def psend(s):
        pr[s] = send(rg.at[s, core], rg.at[s, core], pair)

    zsend(zp, 1, 0, SLOT[-1])
    zsend(zm, -1, 0, SLOT[1])
    psend(0)
    l_qol.wait()
    qo_in = [send(qol.at[me], qol.at[me], at_ctx(*o)) for o in ctx_offsets]
    kv_in = [send(key_h.at[0], kv.at[0, core], pair), send(val_h.at[0], kv.at[1, core], pair)]

    for c in l_w:
        c.wait()
    l_gain.wait()

    @pl.loop(0, WD // 32)
    def _(i):
        rows = pl.ds(pl.multiple_of(i * 32, 32), 32)
        for n in range(2):
            hi, lo = split(w2f[n, rows, :])
            w2h[rows, n * WF : (n + 1) * WF] = hi
            w2l[rows, n * WF : (n + 1) * WF] = lo
        hi, lo = split(wof[rows, :])
        woh[rows, :] = hi
        wol[rows, :] = lo

    @pl.loop(0, WF // 128)
    def _(i):
        rows = pl.ds(pl.multiple_of(i * 128, 128), 128)
        hi, lo = split(wdf[rows, :])
        wdh[rows, :] = hi
        wdl[rows, :] = lo

    zp[SLOT[-1]].wait_recv()
    zsend(zp, 1, SLOT[-1], SLOT[-2])
    psend(SLOT[-1])
    zm[SLOT[1]].wait_recv()
    zsend(zm, -1, SLOT[1], SLOT[2])
    psend(SLOT[1])
    zm[SLOT[2]].wait_recv()
    zsend(zm, -1, SLOT[2], SLOT[3])
    psend(SLOT[2])
    zp[SLOT[-2]].wait_recv()
    zsend(zp, 1, SLOT[-2], SLOT[-3])
    psend(SLOT[-2])

    def project(k):
        both = rg[4 * k : 4 * k + 4]
        resid = both[:, :, 0].reshape(128, WD)
        grad = both[:, :, 1].reshape(128, WD)
        squares = jnp.sum(resid * resid, axis=1, keepdims=True)
        part[k, :, :, :, 2688:] = jnp.broadcast_to(squares, (128, 128)).reshape(4, 4, 8, 128)
        xh, xl = split(resid * gain[...])
        xx = jnp.concatenate([xh, xl], axis=0)
        for n in range(7):
            cols = slice(n * 256, (n + 1) * 256)
            two = nn(xx, w2h[:, cols])
            part[k, :, :, :, cols] = (two[:128] + two[128:] + nn(xh, w2l[:, cols])).reshape(4, 4, 8, 256)
        gh, gl = split(grad)
        gg = jnp.concatenate([gh, gl], axis=0)
        for lo, hi in ((0, 256), (256, 512), (512, 768), (768, 896)):
            two = nt(gg, wdh[lo:hi, :])
            part[k, :, :, :, 1792 + lo : 1792 + hi] = (
                two[:128] + two[128:] + nt(gh, wdl[lo:hi, :])
            ).reshape(4, 4, 8, hi - lo)

    axes = ((at_x, x, at_y, y), (at_y, y, at_x, x))
    cs = (slice(0, HALF), slice(HALF, WIDTH))
    LO, HI = slice(0, 640), slice(640, HALF)

    def wrap(v, o):
        return lax.rem(v + (o + 4), 4)

    def pview(ref, k, h, b, a):
        return ref.at[k, b, a, :, cs[h]] if h == 0 else ref.at[k, a, b, :, cs[h]]

    def pread(ref, k, h, b, a):
        return ref[k, b, a, :, cs[h]] if h == 0 else ref[k, a, b, :, cs[h]]

    B01, B23 = pl.ds(0, 2), pl.ds(2, 2)
    m1, m2 = {}, {}

    def rs1_send(k):
        for h in range(2):
            go, av, _, _ = axes[h]
            m1[k, h, "rp"] = send(pview(part, k, h, B01, wrap(av, 2)), r1.at[k, h, 0], go(1))
            m1[k, h, "rm"] = send(pview(part, k, h, B23, wrap(av, 2)), r1.at[k, h, 1], go(-1))
        for h in range(2):
            go, av, _, _ = axes[h]
            m1[k, h, "dp"] = send(pview(part, k, h, B23, wrap(av, 1)), d1.at[k, h, 0], go(1))
            m1[k, h, "dm"] = send(pview(part, k, h, B01, wrap(av, -1)), d1.at[k, h, 1], go(-1))

    def rs1_relay(k):
        for h in range(2):
            go, av, _, _ = axes[h]
            m1[k, h, "rp"].wait_recv()
            r1[k, h, 0] = r1[k, h, 0] + pread(part, k, h, B01, wrap(av, 1))
            m1[k, h, "cp"] = send(r1.at[k, h, 0], c1.at[k, h, 0], go(1))
            m1[k, h, "rm"].wait_recv()
            r1[k, h, 1] = r1[k, h, 1] + pread(part, k, h, B23, wrap(av, -1))
            m1[k, h, "cm"] = send(r1.at[k, h, 1], c1.at[k, h, 1], go(-1))

    def rs1_final(k):
        for h in range(2):
            _, av, go, bv = axes[h]
            for n in ("dp", "dm", "cp", "cm"):
                m1[k, h, n].wait_recv()
            q1[k, h, 0:2] = pread(part, k, h, B01, av) + c1[k, h, 0] + d1[k, h, 1]
            q1[k, h, 2:4] = pread(part, k, h, B23, av) + d1[k, h, 0] + c1[k, h, 1]
            m2[k, h, "rp"] = send(q1.at[k, h, wrap(bv, 2), :, LO], r2.at[k, h, 0, :, LO], go(1))
            m2[k, h, "rm"] = send(q1.at[k, h, wrap(bv, 2), :, HI], r2.at[k, h, 1, :, HI], go(-1))
            m2[k, h, "dp"] = send(q1.at[k, h, wrap(bv, 1), :, HI], d2.at[k, h, 0, :, HI], go(1))
            m2[k, h, "dm"] = send(q1.at[k, h, wrap(bv, -1), :, LO], d2.at[k, h, 1, :, LO], go(-1))

    def rs2_relay(k):
        for h in range(2):
            _, _, go, bv = axes[h]
            m2[k, h, "rp"].wait_recv()
            r2[k, h, 0, :, LO] = r2[k, h, 0, :, LO] + q1[k, h, wrap(bv, 1), :, LO]
            m2[k, h, "cp"] = send(r2.at[k, h, 0, :, LO], c2.at[k, h, 0, :, LO], go(1))
            m2[k, h, "rm"].wait_recv()
            r2[k, h, 1, :, HI] = r2[k, h, 1, :, HI] + q1[k, h, wrap(bv, -1), :, HI]
            m2[k, h, "cm"] = send(r2.at[k, h, 1, :, HI], c2.at[k, h, 1, :, HI], go(-1))

    def gate(k):
        sums = []
        for h in range(2):
            _, _, _, bv = axes[h]
            for n in ("dp", "dm", "cp", "cm"):
                m2[k, h, n].wait_recv()
            sums.append(q1[k, h, bv, :, LO] + c2[k, h, 0, :, LO] + d2[k, h, 1, :, LO])
            sums.append(q1[k, h, bv, :, HI] + d2[k, h, 0, :, HI] + c2[k, h, 1, :, HI])
        total = jnp.concatenate(sums, axis=1)
        inv = lax.rsqrt(total[:, 2688:] / D + EPS)
        inv1 = inv[:, 0:1]
        gate_raw, up_raw, d_hidden = total[:, 0:896], total[:, 896:1792], total[:, 1792:2688]
        gate_out, up_out = gate_raw * inv1, up_raw * inv1
        sig = jax.nn.sigmoid(gate_out)
        activated = gate_out * sig
        d_up = d_hidden * activated
        d_gate = d_hidden * up_out * sig * (1.0 + gate_out * (1.0 - sig))
        dot = jnp.sum(d_gate * gate_raw + d_up * up_raw, axis=1, keepdims=True)
        coef = inv * inv * inv * dot / D
        lane = lax.broadcasted_iota(jnp.int32, (8, 128), 1)
        full[k, y, x, :, 0:896] = activated * up_out
        full[k, y, x, :, 896:1792] = d_gate
        full[k, y, x, :, 1792:2688] = d_up
        full[k, y, x, :, 2688:] = jnp.where(lane < 64, inv, coef)

    def sub(c, part_of):
        return slice(c.start + part_of.start, c.start + part_of.stop)

    def fview(k, h, b, a, cols=None):
        cols = cs[h] if cols is None else sub(cs[h], cols)
        return full.at[k, b, a, :, cols] if h == 0 else full.at[k, a, b, :, cols]

    def fsend(bag, name, k, h, b, a, dev, cols=None):
        v = fview(k, h, b, a, cols)
        bag[k, h, name] = send(v, v, dev)

    g1, g2 = {}, {}

    def ag1_send(k):
        for h in range(2):
            _, av, go, bv = axes[h]
            fsend(g1, "p", k, h, bv, av, go(1))
            fsend(g1, "m", k, h, bv, av, go(-1))

    def ag1_relay(k):
        for h in range(2):
            _, av, go, bv = axes[h]
            g1[k, h, "p"].wait_recv()
            fsend(g1, "fp", k, h, wrap(bv, -1), av, go(1), LO)
            g1[k, h, "m"].wait_recv()
            fsend(g1, "fm", k, h, wrap(bv, 1), av, go(-1), HI)

    ALL = pl.ds(0, 4)

    def ag2_send(k):
        for h in range(2):
            go, av, _, _ = axes[h]
            g1[k, h, "fp"].wait_recv()
            g1[k, h, "fm"].wait_recv()
            fsend(g2, "p", k, h, ALL, av, go(1))
            fsend(g2, "m", k, h, ALL, av, go(-1))

    def ag2_relay(k):
        for h in range(2):
            go, av, _, _ = axes[h]
            g2[k, h, "p"].wait_recv()
            fsend(g2, "fp", k, h, B01, wrap(av, -1), go(1))
            g2[k, h, "m"].wait_recv()
            fsend(g2, "fm", k, h, B23, wrap(av, 1), go(-1))

    zf = {}
    pf = {}

    def input_grad(k):
        for h in range(2):
            g2[k, h, "fp"].wait_recv()
            g2[k, h, "fm"].wait_recv()
        dgu = full[k, :, :, :, 896:2688].reshape(128, 1792)
        tile = full[k, :, :, :, 2688:].reshape(128, 128)
        inv, coef = tile[:, 0:1], tile[:, 64:65]
        dn = three(dgu, w2h[...], w2l[...], nt)
        resid = rg[4 * k : 4 * k + 4, :, 0].reshape(128, WD)
        t = dn * gain[...] * inv - resid * coef
        tpart[k] = t.reshape(4, 2, BR, WD)
        pf[k] = send(tpart.at[k, :, other], tpair.at[k], pair)

    def input_grad_send(k):
        pf[k].wait_recv()
        usum[k] = tpart[k, :, core] + tpair[k]
        for s in range(4 * k + 3, max(4 * k, 1) - 1, -1):
            zf[s] = send(usum.at[k, s % 4], rz.at[s], at_z(OFF[s]))

    def weight_grads():
        inv = full[:, :, :, :, 2688:].reshape(ROWS, 128)[:, 0:1]
        both = rg[...]
        resid = both[:, :, 0].reshape(ROWS, WD)
        grad = both[:, :, 1].reshape(ROWS, WD)
        nt_ = (resid * gain[...] * inv).T
        nh, nl = split(nt_)
        nn2 = jnp.concatenate([nh, nl], axis=0)
        for n in range(7):
            cols = slice(896 + n * 256, 896 + (n + 1) * 256)
            bh, bl = split(full[:, :, :, :, cols].reshape(ROWS, 256))
            two = nn(nn2, bh)
            gw2[:, n * 256 : (n + 1) * 256] = two[:WD] + two[WD:] + nn(nh, bl)
        gh, gl = split(grad)
        for n in range(7):
            cols = slice(n * 128, (n + 1) * 128)
            ht = full[:, :, :, :, cols].reshape(ROWS, 128).T
            hh, hl = split(ht)
            two = nn(jnp.concatenate([hh, hl], axis=0), gh)
            gwd[cols, :] = two[:128] + two[128:] + nn(hh, gl)

    def attention_split():
        for c in l_kv:
            c.wait()
        for c in kv_in:
            c.wait_recv()

        @pl.loop(0, 16)
        def _(i):
            m, j = i // 8, lax.rem(i, 8)
            src = pl.ds(pl.multiple_of(j * 128, 128), 128)
            dst = pl.ds(pl.multiple_of(i * 128, 128), 128)
            for n, out in ((0, k3), (1, v3)):
                hi, lo = split(kv[n, m, src, :])
                out[dst, 0:128] = hi
                out[dst, 128:256] = lo
                out[dst, 256:384] = hi

    def attention_probs(h):
        q = qol[:, :, h * HD : (h + 1) * HD].reshape(ROWS, HD)
        lse = qol[:, :, 512:].reshape(ROWS, 128)[:, h : h + 1]
        qh, ql = split(q)
        q3 = jnp.concatenate([qh, qh, ql], axis=1)

        @pl.loop(0, 4)
        def _(i):
            keys = pl.ds(pl.multiple_of(i * 512, 512), 512)
            s = nt(q3, k3[keys, :]) * SCALE
            first = (i // 2) * (KEYS * NCTX) + me * KEYS + lax.rem(i, 2) * 512
            pos = first + lax.broadcasted_iota(jnp.int32, (ROWS, 512), 1)
            row = (CONTEXT - ROWS) + lax.broadcasted_iota(jnp.int32, (ROWS, 512), 0)
            probs[h, :, keys] = jnp.where(pos <= row, jnp.exp(s - lse), 0.0)

    def project_first():
        for s in (0, 1, 2, 3):
            pr[s].wait_recv()
        project(0)
        rs1_send(0)

    project_first()
    zm[SLOT[3]].wait_recv()
    zsend(zm, -1, SLOT[3], SLOT[4], 1)
    psend(SLOT[3])
    zp[SLOT[-3]].wait_recv()
    zsend(zp, 1, SLOT[-3], SLOT[4], 0)
    psend(SLOT[-3])
    zm[SLOT[4]].wait_recv()
    zp[SLOT[4]].wait_recv()
    psend(SLOT[4])
    for s in (4, 5, 6, 7):
        pr[s].wait_recv()
    project(1)
    rs1_send(1)
    rs1_relay(0)
    attention_split()
    rs1_relay(1)
    rs1_final(0)
    for c in qo_in:
        c.wait_recv()
    attention_probs(0)
    rs1_final(1)
    rs2_relay(0)
    attention_probs(1)
    rs2_relay(1)
    gate(0)
    ag1_send(0)
    gate(1)
    ag1_send(1)
    ag1_relay(0)
    ag1_relay(1)
    ag2_send(0)
    ag2_send(1)
    ag2_relay(0)
    ag2_relay(1)
    input_grad(0)
    input_grad_send(0)
    input_grad(1)
    input_grad_send(1)
    weight_grads()
    outs = [
        local(gw2.at[:, 0:WF], gwg_o),
        local(gw2.at[:, WF : 2 * WF], gwu_o),
        local(gwd, gwd_o),
    ]

    total = rg[0, core, 1] + usum[0, 0]
    for s in range(1, 8):
        zf[s].wait_recv()
        total = total + rz[s]
    gres[wide] = total
    outs.append(local(gres.at[wide], gres_o))
    gz = {}
    for s in range(7, 0, -1):
        gz[s] = send(gres.at[wide], gres.at[wide], at_z(OFF[s]))
    gp = [send(gres.at[wide], gres.at[wide], pair)]
    for s in range(1, 8):
        gz[s].wait_recv()
        w = 2 * lax.rem(z + (NZ - OFF[s]), NZ) + core
        gp.append(send(gres.at[w], gres.at[w], pair))
    for c in gp:
        c.wait_recv()

    all_gres = gres[...].reshape(ROWS, WD)
    da[...] = three(all_gres, woh[...], wol[...], nt).reshape(16, BR, WD)
    sent = []
    for n, o in enumerate(ctx_offsets):
        sent.append(send(da.at[ctx_of(*o)], rda.at[n], at_ctx(*o)))

    ot = qol[:, :, 256:512].reshape(ROWS, WD).T
    oh, ol = split(ot)
    eh, el = split(all_gres)
    two = nn(jnp.concatenate([oh, ol], axis=0), eh)
    gwo[...] = two[:WD] + two[WD:] + nn(oh, el)
    outs.append(local(gwo, gwo_o))

    own = da[me]
    for n, c in enumerate(sent):
        c.wait_recv()
        own = own + rda[n]
    dat[me] = own
    gat = [send(dat.at[me], dat.at[me], at_ctx(*o)) for o in ctx_offsets]
    for c in gat:
        c.wait_recv()

    for h in range(2):
        d_attn = dat[:, :, h * HD : (h + 1) * HD].reshape(ROWS, HD)
        o = qol[:, :, 256 + h * HD : 256 + (h + 1) * HD].reshape(ROWS, HD)
        delta = jnp.sum(d_attn * o, axis=1, keepdims=True)
        dh, dl = split(d_attn)
        d3 = jnp.concatenate([dh, dh, dl], axis=1)
        acc[...] = jnp.zeros_like(acc)

        @pl.loop(0, 4)
        def _(i):
            keys = pl.ds(pl.multiple_of(i * 512, 512), 512)
            g = probs[h, :, keys] * (nt(d3, v3[keys, :]) - delta)
            gh, gl = split(g)
            acc[...] += nn(jnp.concatenate([gh, gl], axis=0), k3[keys, 0:256])

        a = acc[...]
        out = (a[:ROWS, :HD] + a[:ROWS, HD:] + a[ROWS:, :HD] + a[ROWS:, HD:]) * SCALE
        dq[:, :, h * HD : (h + 1) * HD] = out.reshape(16, BR, HD)

    last = []
    for n, o in enumerate(ctx_offsets):
        last.append(send(dq.at[ctx_of(*o)], rdq.at[n], at_ctx(*o)))
    own = dq[me]
    for n, c in enumerate(last):
        c.wait_recv()
        own = own + rdq[n]
    gqs[...] = own
    outs.append(local(gqs, gq_o))
    for c in started:
        c.wait_send()
    for c in outs:
        c.wait()


def shards(residual, grad_out, norm_gain, w_gate, w_up, w_down, w_out, queries, attn_out, log_sum_exp, key_cache, value_cache):
    lse = jnp.pad(log_sum_exp.T, ((0, 0), (0, 126)))
    qol = jnp.concatenate([queries, attn_out, lse], axis=1)
    V = pltpu.VMEM
    shape = jax.ShapeDtypeStruct
    scratch = [
        V((8, 2, 2, BR, WD), F32),
        V((1, WD), F32),
        V((2, WD, WF), F32), V((WF, WD), F32), V((WD, WD), F32),
        V((WD, 2 * WF), BF16), V((WD, 2 * WF), BF16),
        V((WF, WD), BF16), V((WF, WD), BF16),
        V((WD, WD), BF16), V((WD, WD), BF16),
        V((16, BR, 640), F32),
        V((2, 2, KEYS, HD), F32),
        V((2 * KEYS, 384), BF16), V((2 * KEYS, 384), BF16),
        V((2, 4, 4, 8, WIDTH), F32),
        V((2, 2, 2, 2, 8, HALF), F32), V((2, 2, 2, 2, 8, HALF), F32), V((2, 2, 2, 2, 8, HALF), F32),
        V((2, 2, 4, 8, HALF), F32),
        V((2, 2, 2, 8, HALF), F32), V((2, 2, 2, 8, HALF), F32), V((2, 2, 2, 8, HALF), F32),
        V((2, 4, 4, 8, WIDTH), F32),
        V((2, 4, 2, BR, WD), F32), V((2, 4, BR, WD), F32), V((2, 4, BR, WD), F32),
        V((8, BR, WD), F32),
        V((16, BR, WD), F32), V((16, BR, WD), F32), V((15, BR, WD), F32), V((16, BR, WD), F32),
        V((2, ROWS, 2 * KEYS), F32),
        V((2 * ROWS, 2 * HD), F32),
        V((16, BR, WD), F32), V((15, BR, WD), F32),
        V((WD, 2 * WF), F32), V((WF, WD), F32), V((WD, WD), F32), V((BR, WD), F32),
        pltpu.SemaphoreType.DMA((24,)),
        pltpu.SemaphoreType.DMA((192,)),
        pltpu.SemaphoreType.DMA((192,)),
    ]
    anyspec = pl.BlockSpec(memory_space=pl.ANY)
    return pl.pallas_call(
        kernel,
        out_shape=(
            shape((WD, WF), F32), shape((WD, WF), F32), shape((WF, WD), F32),
            shape((WD, WD), F32), shape((BR, WD), F32), shape((BR, WD), F32),
        ),
        in_specs=[anyspec] * 10,
        out_specs=(anyspec,) * 6,
        scratch_shapes=scratch,
        compiler_params=pltpu.CompilerParams(
            collective_id=0, has_side_effects=True, vmem_limit_bytes=60 * 1024 * 1024
        ),
    )(residual, grad_out, norm_gain.reshape(1, WD), w_gate, w_up, w_down, w_out, qol, key_cache, value_cache)


def solution(mesh):
    torus = Mesh(mesh.devices.reshape(NZ, 2, NY, NX), ("z", "core", "y", "x"))
    wide, ctx = ("z", "core"), ("y", "x")
    return jax.shard_map(
        shards,
        mesh=torus,
        in_specs=(
            P(wide, ctx), P(wide, ctx), P(ctx), P(ctx, wide), P(ctx, wide), P(wide, ctx), P(wide, ctx),
            P(ctx, wide), P(ctx, wide), P(wide, ctx), P(wide, ctx, None), P(wide, ctx, None),
        ),
        out_specs=(P(ctx, wide), P(ctx, wide), P(wide, ctx), P(wide, ctx), P(wide, ctx), P(ctx, wide)),
        check_vma=False,
    )
```

time: 294 us -> 111 us (0.38)
  blocking collectives: 107 us -> 0 us
  Pallas kernels: 0 us -> 101 us
  waiting for transfers between devices: 89.9 us -> 0 us
  matrix products: 40.7 us -> 0 us
  starting transfers between devices: 23.9 us -> 0 us
  between operations: 14.5 us -> 0.66 us
  other arithmetic: 8.64 us -> 1.36 us
    pallas_call x0 -> x1, Pallas kernels: none -> 101 us  [shards(): pl.pallas_call(kernel, out_shape=(shape((WD, WF), F32), shape((WD, WF), F...]
    psum x1 -> x0, waiting for transfers between devices: 67 us -> none  [shards(): lax.psum((matmul(gained, w_gate), matmul(gained, w_up), matmul_nt(all_gra...]
    psum x3 -> x0, blocking collectives: 49 us -> none  [the longest x1 33.9 us: shards(): lax.psum((matmul(gained, w_gate), matmul(gained, w_up), matmul_nt(all_gra...]
    dot_general x16 -> x0, matrix products: 40.7 us -> none  [the longest x8 19 us: matmul_nt(): lax.dot_general(left, right, (((1,), (1,)), ((), ())), precision=highest,...]
    all_gather x2 -> x0, blocking collectives: 39.9 us -> none  [the longest x1 22.7 us: side_by_side(): lax.all_gather(both, axis, axis=dim, tiled=True)]
    all_to_all x3 -> x0, waiting for transfers between devices: 22.9 us -> none  [summed_on_arrival(): lax.all_to_all(pieces, axis, split_axis=0, concat_axis=0, tiled=True)]
    all_to_all x1 -> x0, blocking collectives: 18.1 us -> none  [copy_for_each(): lax.all_to_all(jnp.broadcast_to(x[None], (length, *x.shape)), axis, 0, 0,...]
    all_to_all x3 -> x0, starting transfers between devices: 16.5 us -> none  [summed_on_arrival(): lax.all_to_all(pieces, axis, split_axis=0, concat_axis=0, tiled=True)]
  transfers between devices with their start and end apart: 9 -> 0, of which waited for: 4 -> 0; matrix products, arithmetic and copies ran while one was open for 8% -> 0% of each run, Pallas kernels for 0% -> 0%
where the time goes in v1:
time: 111 us; the launch traced here: 110 us
  Pallas kernels  101 us (91%)
  local copies, waits for them, and re-layouts  7.64 us (7%)
  other arithmetic  1.36 us (1%)
    pallas_call x1, Pallas kernels, shards(): pl.pallas_call(kernel, out_shape=(shape((WD, WF), F32), shape((WD, WF), F...  101 us
    unnamed x19, local copies, waits for them, and re-layouts  7.64 us

profile of v1, /device:TPU:1, one launch (start us, length us, event | category | flops | bytes accessed | tf_op | source)
XLA Modules:
  0.0 110.2 jit_solution(10285130334108117245)
XLA Ops:
  0.6 0.0 copy-start.5
  0.6 0.7 copy-done.5
  1.3 0.1 copy.18
  1.4 1.4 %select_maximum_fusion.qol_h = f32[16,640]{1,0:T(8,128)} fusion(f32[16,2]{1,0:T(8,128)S(1)} %bitcast.2, f32[16,256]{1,0:T(8,128)} %param.20, f32[16,256]{1,0:T(8,128)} %param.19), kind=kLoop, calls=%fused_computation | loop fusion | flops 40960 | bytes 73856 | tf_op jit(solution)/shard_map/concatenate | solution.py:520
  2.8 100.5 %shard_map.163 = (f32[256,896]{1,0:T(8,128)}, f32[256,896]{1,0:T(8,128)}, f32[896,256]{1,0:T(8,128)}, f32[256,256]{1,0:T(8,128)}, f32[16,256]{1,0:T(8,128)}, /*index=5*/f32[16,256]{1,0:T(8,128)}) custom-call(f32[16,256]{1,0:T(8,128)} %resid_h.1, f32[16,256]{1,0:T(8,128)} %grad_h.1, f32[1,256]{1,0:T(1,128)} %bitcast.3, f32[256,896]{1,0:T(8,128)} %wg_h.1, ...), custom_call_target="tpu_custom_call" | custom-call | tf_op jit(solution)/shard_map/pallas_call | solution.py:550
  103.3 0.0 copy-start.1
  103.3 2.2 %copy.25 = f32[256,896]{1,0:T(8,128)} copy(f32[256,896]{1,0:T(8,128)} %get-tuple-element.12) | data formatting | bytes 1835008
  105.6 0.0 copy-done.1
  105.6 0.0 copy-start
  105.6 0.9 copy.26
  106.5 0.6 copy-done
  107.1 0.0 copy-start.2
  107.1 0.9 copy.27
  108.0 0.2 copy-done.2
  108.2 0.0 copy-start.4
  108.2 0.7 copy.28
  108.9 0.0 copy-done.4
  108.9 0.0 copy-start.3
  108.9 0.6 copy.29
  109.5 0.1 copy-done.3
  109.6 0.6 copy.30
Async XLA Ops:
  0.6 0.7 copy-start.5
  103.3 2.3 %copy-start.1 = (f32[256,896]{1,0:T(8,128)S(1)}, f32[256,896]{1,0:T(8,128)}, u32[]{:S(2)}) copy-start(f32[256,896]{1,0:T(8,128)} %get-tuple-element.13) | copy-start | bytes 2752516
  105.6 1.5 %copy-start = (f32[896,256]{1,0:T(8,128)S(1)}, f32[896,256]{1,0:T(8,128)}, u32[]{:S(2)}) copy-start(f32[896,256]{1,0:T(8,128)} %get-tuple-element.14) | copy-start | bytes 2752516
  107.1 1.1 copy-start.2
  108.2 0.7 copy-start.4
  108.9 0.7 copy-start.3

commit v2 on v1

v2 whole, which is shorter than its diff:
```python
import math

import jax
import jax.numpy as jnp
from jax import lax
from jax.experimental import pallas as pl
from jax.experimental.pallas import tpu as pltpu
from jax.sharding import Mesh
from jax.sharding import PartitionSpec as P

MESH = pl.DeviceIdType.MESH
F32 = jnp.float32
BF16 = jnp.bfloat16
EPS = 1e-05
NZ, NX, NY = 8, 4, 4
NCTX = NX * NY
OFF = (0, 1, -1, 2, -2, 3, -3, 4)
SLOT = {o: s for s, o in enumerate(OFF)}
D, FF, HD = 4096, 14336, 128
WD, WF = D // NCTX, FF // 16
ROWS, BR = 256, 16
HALF = 11 * 128
WIDTH = 2 * HALF
KEYS = 1024
LIMIT = 48 * 1024 * 1024
CONTEXT = 32768
SCALE = 1.0 / math.sqrt(HD)


def split(v):
    hi = v.astype(BF16)
    return hi, (v - hi.astype(F32)).astype(BF16)


def nn(a, b):
    return lax.dot_general(a, b, (((1,), (0,)), ((), ())), preferred_element_type=F32)


def nt(a, b):
    return lax.dot_general(a, b, (((1,), (1,)), ((), ())), preferred_element_type=F32)


def three(a, bh, bl, dot):
    ah, al = split(a)
    m = a.shape[0]
    both = dot(jnp.concatenate([ah, al], axis=0), bh)
    return both[:m] + both[m:] + dot(ah, bl)


def kernel(
    resid_h, grad_h, gain_h, wg_h, wu_h, wd_h, wo_h, q_h, o_h, lse_h, key_h, val_h,
    gwg_o, gwu_o, gwd_o, gwo_o, gres_o, gq_o,
    rg, gain, lse_v, w2f, wdf, wof, w2h, w2l, wdh, wdl, woh, wol, qol, kv, k3, v3,
    part, r1, c1, q1, r2, c2, full, tpart, tpair, usum, rz, gres, da, rda, dat,
    probs, acc, dq, rdq, gw2, gwd, gwo, gqs,
    lsem, ssem, rsem,
):
    z, core = lax.axis_index("z"), lax.axis_index("core")
    y, x = lax.axis_index("y"), lax.axis_index("x")
    me = y * NX + x
    other = 1 - core
    wide = 2 * z + core

    counter = {"l": 0}
    out_at, in_at = {}, {}

    def local(src, dst):
        copy = pltpu.make_async_copy(src, dst, lsem.at[counter["l"]])
        counter["l"] += 1
        copy.start()
        return copy

    def transfer(src, dst, out, into, dev):
        return pltpu.make_async_remote_copy(
            src_ref=src, dst_ref=dst,
            send_sem=ssem.at[out_at.setdefault(out, len(out_at))],
            recv_sem=rsem.at[in_at.setdefault(into, len(in_at))],
            device_id=dev, device_id_type=MESH,
        )

    def send(src, dst, dev, out, into):
        copy = transfer(src, dst, out, into, dev)
        copy.start()
        return copy

    def arrived(into, like):
        transfer(like, like, next(iter(out_at)), into, pair).wait_recv()

    def gone(out, like):
        transfer(like, like, out, next(iter(in_at)), pair).wait_send()

    def at_z(o):
        return {"z": lax.rem(z + (o + NZ), NZ)}

    def at_x(o):
        return {"x": lax.rem(x + (o + NX), NX)}

    def at_y(o):
        return {"y": lax.rem(y + (o + NY), NY)}

    pair = {"core": other}
    ctx_offsets = sorted(
        [(dy, dx) for dy in range(NY) for dx in range(NX) if (dy, dx) != (0, 0)],
        key=lambda o: -(min(o[0], 4 - o[0]) + min(o[1], 4 - o[1])),
    )

    def at_ctx(dy, dx):
        return {"y": lax.rem(y + dy, NY), "x": lax.rem(x + dx, NX)}

    def ctx_of(dy, dx):
        return lax.rem(y + dy, NY) * NX + lax.rem(x + dx, NX)

    l_rg = [local(resid_h, rg.at[0, core, 0]), local(grad_h, rg.at[0, core, 1])]
    l_lse = local(lse_h, lse_v)
    l_w = [local(wg_h, w2f.at[0]), local(wu_h, w2f.at[1])]
    l_wd = [local(wd_h, wdf), local(wo_h, wof), local(gain_h, gain)]
    l_qol = [local(q_h, qol.at[me, :, 0:256]), local(o_h, qol.at[me, :, 256:512])]
    l_kv = [local(key_h.at[0], kv.at[0, core]), local(val_h.at[0], kv.at[1, core])]

    barrier = pltpu.get_barrier_semaphore()
    peers = [pair] + [go(o) for go in (at_z, at_y, at_x) for o in (1, -1)]
    for dev in peers:
        pl.semaphore_signal(barrier, inc=1, device_id=dev, device_id_type=MESH)

    diag = lax.broadcasted_iota(jnp.int32, (BR, BR), 0) == lax.broadcasted_iota(jnp.int32, (BR, BR), 1)
    lane = lax.broadcasted_iota(jnp.int32, (BR, 128), 1)
    l_lse.wait()
    turned = [
        jnp.sum(jnp.where(diag, jnp.broadcast_to(lse_v[h : h + 1, :], (BR, BR)), 0.0), axis=1, keepdims=True)
        for h in range(2)
    ]
    qol[me, :, 512:] = jnp.where(lane == 0, turned[0], turned[1])

    for c in l_w:
        c.wait()

    @pl.loop(0, WD // 32)
    def _(i):
        rows = pl.ds(pl.multiple_of(i * 32, 32), 32)
        for n in range(2):
            hi, lo = split(w2f[n, rows, :])
            w2h[rows, n * WF : (n + 1) * WF] = hi
            w2l[rows, n * WF : (n + 1) * WF] = lo

    pl.semaphore_wait(barrier, len(peers))

    for c in l_rg:
        c.wait()
    zin, pr = {}, {}

    def zsend(s_from, s_to):
        o = 1 if s_to in (2, 4, 6) else -1
        zin[s_to] = send(rg.at[s_from, core], rg.at[s_to, core], at_z(o), "z", ("z", s_to))

    def psend(s):
        pr[s] = send(rg.at[s, core], rg.at[s, core], pair, "pair", ("pair", s))

    zsend(0, 1)
    zsend(0, 2)
    psend(0)
    for c in l_wd:
        c.wait()

    @pl.loop(0, WF // 128)
    def _(i):
        rows = pl.ds(pl.multiple_of(i * 128, 128), 128)
        hi, lo = split(wdf[rows, :])
        wdh[rows, :] = hi
        wdl[rows, :] = lo

    def rows_pass(*slots):
        for s in slots:
            zin[s].wait_recv()
            if s < 6:
                zsend(s, s + 2)
            psend(s)

    rows_pass(1, 2, 3)

    @pl.loop(0, WD // 64)
    def _(i):
        rows = pl.ds(pl.multiple_of(i * 64, 64), 64)
        hi, lo = split(wof[rows, :])
        woh[rows, :] = hi
        wol[rows, :] = lo

    def project(k):
        both = rg[4 * k : 4 * k + 4]
        resid = both[:, :, 0].reshape(128, WD)
        grad = both[:, :, 1].reshape(128, WD)
        squares = jnp.sum(resid * resid, axis=1, keepdims=True)
        part[k, :, :, :, 2688:] = jnp.broadcast_to(squares, (128, 128)).reshape(4, 4, 8, 128)
        xh, xl = split(resid * gain[...])
        xx = jnp.concatenate([xh, xl], axis=0)
        for n in range(7):
            cols = slice(n * 256, (n + 1) * 256)
            two = nn(xx, w2h[:, cols])
            part[k, :, :, :, cols] = (two[:128] + two[128:] + nn(xh, w2l[:, cols])).reshape(4, 4, 8, 256)
        gh, gl = split(grad)
        gg = jnp.concatenate([gh, gl], axis=0)
        for lo, hi in ((0, 256), (256, 512), (512, 768), (768, 896)):
            two = nt(gg, wdh[lo:hi, :])
            part[k, :, :, :, 1792 + lo : 1792 + hi] = (
                two[:128] + two[128:] + nt(gh, wdl[lo:hi, :])
            ).reshape(4, 4, 8, hi - lo)

    axes = ((at_x, x, at_y, y), (at_y, y, at_x, x))
    cs = (slice(0, HALF), slice(HALF, WIDTH))
    LO, HI = slice(0, 640), slice(640, HALF)

    def wrap(v, o):
        return lax.rem(v + (o + 4), 4)

    VIA = {2: 1, 1: -1, 0: 1, 3: -1}

    def at_piece(k, h, r, a):
        b = wrap(axes[h][3], r)
        return (k, b, a, slice(None), cs[h]) if h == 0 else (k, a, b, slice(None), cs[h])

    m1, m2 = {}, {}

    def rs1_send(k):
        for r in (2, 1, 0, 3):
            for h in range(2):
                go, av, _, _ = axes[h]
                m1[k, h, r] = send(
                    part.at[at_piece(k, h, r, wrap(av, 2))], r1.at[k, h, r], go(VIA[r]), "rs1r", ("r", k, h, r)
                )

    def rs1_direct(k):
        for r in (2, 1, 3, 0):
            for h in range(2):
                go, av, _, _ = axes[h]
                send(
                    part.at[at_piece(k, h, r, wrap(av, -VIA[r]))], c1.at[k, h, r, 1], go(-VIA[r]), "rs1d", ("c", k, h, r)
                )

    def rs1_relay(k):
        for r in (2, 1, 0, 3):
            for h in range(2):
                go, av, _, _ = axes[h]
                m1[k, h, r].wait_recv()
                r1[k, h, r] = r1[k, h, r] + part[at_piece(k, h, r, wrap(av, VIA[r]))]
                send(r1.at[k, h, r], c1.at[k, h, r, 0], go(VIA[r]), "rs1c", ("c", k, h, r))

    def rs1_final(k):
        for r in (2, 1, 3, 0):
            for h in range(2):
                _, av, go, _ = axes[h]
                arrived(("c", k, h, r), c1.at[k, h, r])
                q1[k, h, r] = part[at_piece(k, h, r, av)] + c1[k, h, r, 0] + c1[k, h, r, 1]
                if r == 2:
                    m2[k, h, 1] = send(
                        q1.at[k, h, 2, :, LO], r2.at[k, h, 0, :, LO], go(1), "rs2", ("rp", k, h)
                    )
                    m2[k, h, -1] = send(
                        q1.at[k, h, 2, :, HI], r2.at[k, h, 1, :, HI], go(-1), "rs2", ("rm", k, h)
                    )
                elif r == 1:
                    send(q1.at[k, h, 1, :, HI], c2.at[k, h, 0, :, HI], go(1), "rs2", ("c2", k, h))
                elif r == 3:
                    send(q1.at[k, h, 3, :, LO], c2.at[k, h, 1, :, LO], go(-1), "rs2", ("c2", k, h))

    def rs2_relay(k):
        for h in range(2):
            _, _, go, _ = axes[h]
            m2[k, h, 1].wait_recv()
            r2[k, h, 0, :, LO] = r2[k, h, 0, :, LO] + q1[k, h, 1, :, LO]
            send(r2.at[k, h, 0, :, LO], c2.at[k, h, 0, :, LO], go(1), "rs2", ("c2", k, h))
            m2[k, h, -1].wait_recv()
            r2[k, h, 1, :, HI] = r2[k, h, 1, :, HI] + q1[k, h, 3, :, HI]
            send(r2.at[k, h, 1, :, HI], c2.at[k, h, 1, :, HI], go(-1), "rs2", ("c2", k, h))

    def gate(k):
        sums = []
        for h in range(2):
            arrived(("c2", k, h), c2.at[k, h])
            sums.append(q1[k, h, 0] + c2[k, h, 0] + c2[k, h, 1])
        total = jnp.concatenate(sums, axis=1)
        inv = lax.rsqrt(total[:, 2688:] / D + EPS)
        inv1 = inv[:, 0:1]
        gate_raw, up_raw, d_hidden = total[:, 0:896], total[:, 896:1792], total[:, 1792:2688]
        gate_out, up_out = gate_raw * inv1, up_raw * inv1
        sig = jax.nn.sigmoid(gate_out)
        activated = gate_out * sig
        d_up = d_hidden * activated
        d_gate = d_hidden * up_out * sig * (1.0 + gate_out * (1.0 - sig))
        dot = jnp.sum(d_gate * gate_raw + d_up * up_raw, axis=1, keepdims=True)
        coef = inv * inv * inv * dot / D
        lane = lax.broadcasted_iota(jnp.int32, (8, 128), 1)
        full[k, y, x, :, 0:896] = activated * up_out
        full[k, y, x, :, 896:1792] = d_gate
        full[k, y, x, :, 1792:2688] = d_up
        full[k, y, x, :, 2688:] = jnp.where(lane < 64, inv, coef)

    def sub(c, part_of):
        return slice(c.start + part_of.start, c.start + part_of.stop)

    def fsend(k, h, r, a, dev, out, into, cols=None):
        at = at_piece(k, h, r, a)
        if cols is not None:
            at = at[:-1] + (sub(cs[h], cols),)
        return send(full.at[at], full.at[at], dev, out, into)

    g1, g2 = {}, {}

    def ag_across(k, h, r):
        go, av, _, _ = axes[h]
        for d in (1, -1):
            into = ("a", k, h, r) if d == VIA[r] else ("done", k)
            g2[k, h, r, d] = fsend(k, h, r, av, go(d), ("a", k), into)

    def ag_own(k):
        for h in range(2):
            _, av, go, _ = axes[h]
            for d in (1, -1):
                g1[k, h, d] = fsend(k, h, 0, av, go(d), "ag1", ("b", k, h, d))
        for h in range(2):
            ag_across(k, h, 0)

    def ag_near(k):
        for h in range(2):
            _, av, go, _ = axes[h]
            g1[k, h, 1].wait_recv()
            fsend(k, h, 3, av, go(1), "ag1", ("b2", k, h), LO)
            g1[k, h, -1].wait_recv()
            fsend(k, h, 1, av, go(-1), "ag1", ("b2", k, h), HI)
        for r in (3, 1):
            for h in range(2):
                ag_across(k, h, r)

    def ag_far(k):
        for h in range(2):
            arrived(("b2", k, h), q1.at[k, h, 0])
            ag_across(k, h, 2)

    def ag_pass(k, r):
        for h in range(2):
            go, av, _, _ = axes[h]
            g2[k, h, r, VIA[r]].wait_recv()
            fsend(k, h, r, wrap(av, -VIA[r]), go(VIA[r]), "pass", ("done", k))

    def ag_done(k):
        arrived(("done", k), full.at[k, :, :, :, cs[0]])

    pf = {}

    def input_grad(k):
        ag_done(k)
        dgu = full[k, :, :, :, 896:2688].reshape(128, 1792)
        tile = full[k, :, :, :, 2688:].reshape(128, 128)
        inv, coef = tile[:, 0:1], tile[:, 64:65]
        dn = three(dgu, w2h[...], w2l[...], nt)
        resid = rg[4 * k : 4 * k + 4, :, 0].reshape(128, WD)
        t = dn * gain[...] * inv - resid * coef
        tpart[k] = t.reshape(4, 2, BR, WD)
        pf[k] = send(tpart.at[k, :, other], tpair.at[k], pair, "pf", ("pf", k))

    def input_grad_send(k):
        pf[k].wait_recv()
        usum[k] = tpart[k, :, core] + tpair[k]
        for s in range(4 * k + 3, max(4 * k, 1) - 1, -1):
            send(usum.at[k, s % 4], rz.at[s], at_z(OFF[s]), "zf", "zf")

    def weight_grads():
        inv = full[:, :, :, :, 2688:].reshape(ROWS, 128)[:, 0:1]
        both = rg[...]
        resid = both[:, :, 0].reshape(ROWS, WD)
        grad = both[:, :, 1].reshape(ROWS, WD)
        nt_ = (resid * gain[...] * inv).T
        nh, nl = split(nt_)
        nn2 = jnp.concatenate([nh, nl], axis=0)
        for n in range(7):
            cols = slice(896 + n * 256, 896 + (n + 1) * 256)
            bh, bl = split(full[:, :, :, :, cols].reshape(ROWS, 256))
            two = nn(nn2, bh)
            gw2[:, n * 256 : (n + 1) * 256] = two[:WD] + two[WD:] + nn(nh, bl)
        gh, gl = split(grad)
        for n in range(7):
            cols = slice(n * 128, (n + 1) * 128)
            ht = full[:, :, :, :, cols].reshape(ROWS, 128).T
            hh, hl = split(ht)
            two = nn(jnp.concatenate([hh, hl], axis=0), gh)
            gwd[cols, :] = two[:128] + two[128:] + nn(hh, gl)

    def attention_split():
        for c in l_kv:
            c.wait()
        arrived("kv", kv.at[:, 0])

        @pl.loop(0, 16)
        def _(i):
            m, j = i // 8, lax.rem(i, 8)
            src = pl.ds(pl.multiple_of(j * 128, 128), 128)
            dst = pl.ds(pl.multiple_of(i * 128, 128), 128)
            for n, out in ((0, k3), (1, v3)):
                hi, lo = split(kv[n, m, src, :])
                out[dst, 0:128] = hi
                out[dst, 128:256] = lo
                out[dst, 256:384] = hi

    def attention_probs(h):
        q = qol[:, :, h * HD : (h + 1) * HD].reshape(ROWS, HD)
        lse = qol[:, :, 512:].reshape(ROWS, 128)[:, h : h + 1]
        qh, ql = split(q)
        q3 = jnp.concatenate([qh, qh, ql], axis=1)

        @pl.loop(0, 4)
        def _(i):
            keys = pl.ds(pl.multiple_of(i * 512, 512), 512)
            s = nt(q3, k3[keys, :]) * SCALE
            first = (i // 2) * (KEYS * NCTX) + me * KEYS + lax.rem(i, 2) * 512
            pos = first + lax.broadcasted_iota(jnp.int32, (ROWS, 512), 1)
            row = (CONTEXT - ROWS) + lax.broadcasted_iota(jnp.int32, (ROWS, 512), 0)
            probs[h, :, keys] = jnp.where(pos <= row, jnp.exp(s - lse), 0.0)

    def rows_pair(k):
        for s in range(4 * k, 4 * k + 4):
            pr[s].wait_recv()

    outs = []

    def start_kv():
        send(key_h.at[0], kv.at[0, core], pair, "kv", "kv")
        send(val_h.at[0], kv.at[1, core], pair, "kv", "kv")

    def start_qo():
        for c in l_qol:
            c.wait()
        for o in ctx_offsets:
            send(qol.at[me], qol.at[me], at_ctx(*o), "qo", "qo")

    gz = {}

    def resid_own():
        total = rg[0, core, 1] + usum[0, 0]
        arrived("zf", rz.at[1:8])
        for s in range(1, 8):
            total = total + rz[s]
        gres[wide] = total
        for s in range(7, 0, -1):
            gz[s] = send(gres.at[wide], gres.at[wide], at_z(OFF[s]), "g", ("g", s))
        send(gres.at[wide], gres.at[wide], pair, "g", "gp")
        outs.append(local(gres.at[wide], gres_o))

    def resid_all():
        for s in range(1, 8):
            gz[s].wait_recv()
            w = 2 * lax.rem(z + (NZ - OFF[s]), NZ) + core
            send(gres.at[w], gres.at[w], pair, "g", "gp")

    def resid_pair():
        arrived("gp", gres.at[0:8])

    def d_attn_part():
        gh, gl = split(gres[...].reshape(ROWS, WD))
        gg = jnp.concatenate([gh, gl], axis=0)
        for h in range(2):
            cols = slice(h * HD, (h + 1) * HD)
            two = nt(gg, woh[cols, :])
            da[h] = (two[:ROWS] + two[ROWS:] + nt(gh, wol[cols, :])).reshape(16, BR, HD)
            for n, o in enumerate(ctx_offsets):
                send(da.at[h, ctx_of(*o)], rda.at[h, n], at_ctx(*o), "di", ("di", h))

    def out_grad():
        oh, ol = split(qol[:, :, 256:512].reshape(ROWS, WD).T)
        eh, el = split(gres[...].reshape(ROWS, WD))
        two = nn(jnp.concatenate([oh, ol], axis=0), eh)
        gwo[...] = two[:WD] + two[WD:] + nn(oh, el)
        outs.append(local(gwo, gwo_o))

    def d_attn_sum(h):
        arrived(("di", h), rda.at[h])
        own = da[h, me]
        for n in range(NCTX - 1):
            own = own + rda[h, n]
        dat[h, me] = own
        for o in ctx_offsets:
            send(dat.at[h, me], dat.at[h, me], at_ctx(*o), "do", ("do", h))

    def d_attn_all(h):
        arrived(("do", h), rda.at[h])

    def query_grad(h):
        d_attn = dat[h].reshape(ROWS, HD)
        o = qol[:, :, 256 + h * HD : 256 + (h + 1) * HD].reshape(ROWS, HD)
        delta = jnp.sum(d_attn * o, axis=1, keepdims=True)
        dh, dl = split(d_attn)
        d3 = jnp.concatenate([dh, dh, dl], axis=1)
        acc[...] = jnp.zeros_like(acc)

        for i in range(4):
            keys = slice(i * 512, (i + 1) * 512)
            g = probs[h, :, keys] * (nt(d3, v3[keys, :]) - delta)
            gh, gl = split(g)
            acc[...] += nn(jnp.concatenate([gh, gl], axis=0), k3[keys, 0:256])

        a = acc[...]
        out = (a[:ROWS, :HD] + a[:ROWS, HD:] + a[ROWS:, :HD] + a[ROWS:, HD:]) * SCALE
        dq[h] = out.reshape(16, BR, HD)
        for n, o in enumerate(ctx_offsets):
            send(dq.at[h, ctx_of(*o)], rdq.at[h, n], at_ctx(*o), "qi", ("qi", h))

    def query_sum(h):
        arrived(("qi", h), rdq.at[h])
        own = dq[h, me]
        for n in range(NCTX - 1):
            own = own + rdq[h, n]
        gqs[:, h * HD : (h + 1) * HD] = own

    def store_weights():
        outs.append(local(gw2.at[:, 0:WF], gwg_o))
        outs.append(local(gw2.at[:, WF : 2 * WF], gwu_o))
        outs.append(local(gwd, gwd_o))

    def qo_wait():
        arrived("qo", qol.at[0:15])

    def finish():
        outs.append(local(gqs, gq_o))
        sixteen = full.at[0, :, :, :, cs[0]]
        for out, like in (
            ("z", rg.at[1:8, 0]), ("pair", rg.at[:, 0]), ("kv", kv.at[:, 0]), ("qo", qol.at[0:15]),
            ("rs1r", sixteen), ("rs1d", sixteen), ("rs1c", sixteen), ("rs2", q1.at[:, :, 0:3]),
            ("ag1", q1.at[:, :, 0:3]), (("a", 0), sixteen), (("a", 1), sixteen), ("pass", sixteen),
            ("pf", tpair), ("zf", rz.at[1:8]), ("g", gres.at[0:15]), ("di", rda), ("do", rda), ("qi", rdq),
        ):
            gone(out, like)
        for c in outs:
            c.wait()

    rows_pair(0)
    project(0)
    rs1_send(0)
    rs1_direct(0)
    rows_pass(4, 5, 6)
    rs1_relay(0)
    rows_pass(7)
    rows_pair(1)
    project(1)
    rs1_send(1)
    rs1_final(0)
    rs1_direct(1)
    start_kv()
    rs2_relay(0)
    rs1_relay(1)
    gate(0)
    ag_own(0)
    rs1_final(1)
    ag_near(0)
    ag_pass(0, 0)
    rs2_relay(1)
    ag_far(0)
    gate(1)
    ag_own(1)
    ag_pass(0, 3)
    ag_pass(0, 1)
    ag_near(1)
    ag_pass(0, 2)
    ag_pass(1, 0)
    ag_far(1)
    ag_pass(1, 3)
    ag_pass(1, 1)
    ag_pass(1, 2)
    input_grad(0)
    input_grad_send(0)
    input_grad(1)
    input_grad_send(1)
    start_qo()
    weight_grads()
    store_weights()
    attention_split()
    resid_own()
    resid_all()
    resid_pair()
    d_attn_part()
    qo_wait()
    out_grad()
    attention_probs(0)
    d_attn_sum(0)
    d_attn_sum(1)
    attention_probs(1)
    d_attn_all(0)
    query_grad(0)
    d_attn_all(1)
    query_grad(1)
    query_sum(0)
    query_sum(1)
    finish()


def put(*refs):
    sem = refs[12]
    copies = [pltpu.make_async_copy(refs[n], refs[6 + n], sem.at[n]) for n in range(6)]
    for c in copies:
        c.start()
    for c in copies:
        c.wait()


def shards(residual, grad_out, norm_gain, w_gate, w_up, w_down, w_out, queries, attn_out, log_sum_exp, key_cache, value_cache):
    operands = (
        residual, grad_out, norm_gain.reshape(1, WD), w_gate, w_up, w_down, w_out,
        queries, attn_out, log_sum_exp, key_cache, value_cache,
    )
    V = pltpu.VMEM
    shape = jax.ShapeDtypeStruct
    scratch = [
        V((8, 2, 2, BR, WD), F32),
        V((1, WD), F32), V((2, BR), F32),
        V((2, WD, WF), F32), V((WF, WD), F32), V((WD, WD), F32),
        V((WD, 2 * WF), BF16), V((WD, 2 * WF), BF16),
        V((WF, WD), BF16), V((WF, WD), BF16),
        V((WD, WD), BF16), V((WD, WD), BF16),
        V((16, BR, 640), F32),
        V((2, 2, KEYS, HD), F32),
        V((2 * KEYS, 384), BF16), V((2 * KEYS, 384), BF16),
        V((2, 4, 4, 8, WIDTH), F32),
        V((2, 2, 4, 8, HALF), F32), V((2, 2, 4, 2, 8, HALF), F32),
        V((2, 2, 4, 8, HALF), F32),
        V((2, 2, 2, 8, HALF), F32), V((2, 2, 2, 8, HALF), F32),
        V((2, 4, 4, 8, WIDTH), F32),
        V((2, 4, 2, BR, WD), F32), V((2, 4, BR, WD), F32), V((2, 4, BR, WD), F32),
        V((8, BR, WD), F32),
        V((16, BR, WD), F32), V((2, 16, BR, HD), F32), V((2, 15, BR, HD), F32), V((2, 16, BR, HD), F32),
        V((2, ROWS, 2 * KEYS), F32),
        V((2 * ROWS, 2 * HD), F32),
        V((2, 16, BR, HD), F32), V((2, 15, BR, HD), F32),
        V((WD, 2 * WF), F32), V((WF, WD), F32), V((WD, WD), F32), V((BR, WD), F32),
        pltpu.SemaphoreType.DMA((18,)),
        pltpu.SemaphoreType.DMA((18,)),
        pltpu.SemaphoreType.DMA((108,)),
    ]
    hbm = pl.BlockSpec(memory_space=pltpu.HBM)
    anyspec = pl.BlockSpec(memory_space=pl.ANY)
    sent = pl.pallas_call(
        kernel,
        out_shape=(
            shape((WD, WF), F32), shape((WD, WF), F32), shape((WF, WD), F32),
            shape((WD, WD), F32), shape((BR, WD), F32), shape((BR, WD), F32),
        ),
        in_specs=[hbm] * 12,
        out_specs=(anyspec,) * 6,
        scratch_shapes=scratch,
        compiler_params=pltpu.CompilerParams(
            collective_id=0, has_side_effects=True, vmem_limit_bytes=LIMIT
        ),
    )(*[pltpu.with_memory_space_constraint(a, pltpu.HBM) for a in operands])
    return pl.pallas_call(
        put,
        out_shape=tuple(shape(o.shape, F32) for o in sent),
        in_specs=[anyspec] * 6,
        out_specs=(hbm,) * 6,
        scratch_shapes=[pltpu.SemaphoreType.DMA((6,))],
        compiler_params=pltpu.CompilerParams(vmem_limit_bytes=1024 * 1024),
    )(*sent)


def solution(mesh):
    torus = Mesh(mesh.devices.reshape(NZ, 2, NY, NX), ("z", "core", "y", "x"))
    wide, ctx = ("z", "core"), ("y", "x")
    return jax.shard_map(
        shards,
        mesh=torus,
        in_specs=(
            P(wide, ctx), P(wide, ctx), P(ctx), P(ctx, wide), P(ctx, wide), P(wide, ctx), P(wide, ctx),
            P(ctx, wide), P(ctx, wide), P(wide, ctx), P(wide, ctx, None), P(wide, ctx, None),
        ),
        out_specs=(P(ctx, wide), P(ctx, wide), P(wide, ctx), P(wide, ctx), P(wide, ctx), P(ctx, wide)),
        check_vma=False,
    )
```

time: 111 us -> 91 us (0.82)
  Pallas kernels: 101 us -> 90.3 us
  local copies, waits for them, and re-layouts: 7.64 us -> 0 us
  other arithmetic: 1.36 us -> 0 us
    pallas_call x1, Pallas kernels: 101 us -> 88.6 us  [shards(): pl.pallas_call(kernel, out_shape=(shape((WD, WF), F32), shape((WD, WF), F...]
    unnamed x19 -> x0, local copies, waits for them, and re-layouts: 7.64 us -> none
    pallas_call x0 -> x1, Pallas kernels: none -> 1.67 us  [shards(): pl.pallas_call(put, out_shape=tuple((shape(o.shape, F32) for o in sent)),...]
    concatenate x1 -> x0, other arithmetic: 1.36 us -> none  [shards(): qol = jnp.concatenate([queries, attn_out, lse], axis=1)]
where the time goes in v2:
time: 91 us; the launch traced here: 90.9 us
  Pallas kernels  90.3 us (99%)
    pallas_call x1, Pallas kernels, shards(): pl.pallas_call(kernel, out_shape=(shape((WD, WF), F32), shape((WD, WF), F...  88.6 us

profile of v2, /device:TPU:1, one launch (start us, length us, event | category | flops | bytes accessed | tf_op | source)
XLA Modules:
  0.0 90.9 jit_solution(1020400501710581277)
XLA Ops:
  0.6 88.6 %shard_map.163 = (f32[256,896]{1,0:T(8,128)S(1)}, f32[256,896]{1,0:T(8,128)S(1)}, f32[896,256]{1,0:T(8,128)S(1)}, f32[256,256]{1,0:T(8,128)S(1)}, f32[16,256]{1,0:T(8,128)S(1)}, /*index=5*/f32[16,256]{1,0:T(8,128)S(1)}) custom-call(f32[16,256]{1,0:T(8,128)} %resid_h.1, f32[16,256]{1,0:T(8,128)} %grad_h.1, f32[1,256]{1,0:T(1,128)} %bitcast.1, ...), custom_call_target="tpu_custom_call" | custom-call | tf_op jit(solution)/shard_map/pallas_call | solution.py:636
  89.3 1.7 %shard_map.164 = (f32[256,896]{1,0:T(8,128)}, f32[256,896]{1,0:T(8,128)}, f32[896,256]{1,0:T(8,128)}, f32[256,256]{1,0:T(8,128)}, f32[16,256]{1,0:T(8,128)}, /*index=5*/f32[16,256]{1,0:T(8,128)}) custom-call(f32[256,896]{1,0:T(8,128)S(1)} %get-tuple-element.12.refs_0_, f32[256,896]{1,0:T(8,128)S(1)} %get-tuple-element.13.refs_1_, ...), custom_call_target="tpu_custom_call" | custom-call | tf_op jit(solution)/shard_map/pallas_call | solution.py:649

commit v3 on v2

--- a/solution.py
+++ b/solution.py
@@ -22,9 +22,35 @@
 HALF = 11 * 128
 WIDTH = 2 * HALF
 KEYS = 1024
+NSEM = 122
 LIMIT = 48 * 1024 * 1024
 CONTEXT = 32768
 SCALE = 1.0 / math.sqrt(HD)
+
+ORDER = (
+    ("S", 0, 0, 2), ("D", 0, 1, 2), ("S", 0, 1, 2), ("D", 0, 0, 2), ("S", 0, 0, 1), ("S", 0, 0, 0), ("D", 0, 0, 3),
+    ("D", 0, 0, 1), ("S", 0, 0, 3), ("D", 0, 0, 0), ("S", 0, 1, 0), ("S", 0, 1, 1), ("D", 0, 1, 3), ("S", 0, 1, 3),
+    ("D", 0, 1, 1), ("D", 0, 1, 0), ("Z", 4), ("Z", 5, 6), ("R", 0, 0, 2), ("R", 0, 1, 2), ("R", 0, 0, 0), ("R", 0, 0, 1),
+    ("R", 0, 1, 1), ("R", 0, 1, 0), ("R", 0, 0, 3), ("R", 0, 1, 3), ("Z", 7), ("J", 1), ("S", 1, 0, 3), ("S", 1, 1, 3),
+    ("S", 1, 1, 2), ("S", 1, 0, 2), ("F", 0, 0, 2), ("F", 0, 1, 2), ("S", 1, 1, 0), ("D", 1, 1, 2), ("S", 1, 0, 1),
+    ("D", 1, 1, 3), ("S", 1, 1, 1), ("S", 1, 0, 0), ("D", 1, 0, 3), ("D", 1, 1, 0), ("D", 1, 0, 2), ("F", 0, 0, 1),
+    ("F", 0, 1, 1), ("F", 0, 1, 3), ("F", 0, 0, 0), ("F", 0, 0, 3), ("R", 1, 1, 2), ("R", 1, 0, 2), ("R", 1, 0, 3),
+    ("T", 0, 1, -1), ("T", 0, 0, -1), ("T", 0, 1, 1), ("T", 0, 0, 1), ("D", 1, 1, 1), ("D", 1, 0, 1), ("R", 1, 1, 3),
+    ("R", 1, 0, 1), ("D", 1, 0, 0), ("R", 1, 0, 0), ("F", 0, 1, 0), ("R", 1, 1, 1), ("R", 1, 1, 0), ("F", 1, 1, 2),
+    ("F", 1, 0, 2), ("G", 0), ("O", 0, 1, 1), ("O", 0, 1, -1), ("O", 0, 0, -1), ("O", 0, 0, 1), ("A", 0, 1, 0, -1),
+    ("A", 0, 1, 0, 1), ("F", 1, 0, 1), ("A", 0, 0, 0, 1), ("A", 0, 0, 0, -1), ("F", 1, 1, 3), ("F", 1, 1, 1),
+    ("F", 1, 0, 3), ("T", 1, 1, -1), ("T", 1, 0, -1), ("T", 1, 0, 1), ("T", 1, 1, 1), ("A", 0, 1, 3, 1),
+    ("N", 0, 1, 1), ("N", 0, 0, -1), ("A", 0, 1, 3, -1), ("N", 0, 1, -1), ("A", 0, 0, 3, -1), ("A", 0, 1, 1, -1),
+    ("A", 0, 0, 1, -1), ("F", 1, 1, 0), ("N", 0, 0, 1), ("A", 0, 1, 1, 1), ("A", 0, 0, 3, 1), ("F", 1, 0, 0),
+    ("A", 0, 0, 1, 1), ("G", 1), ("O", 1, 0, -1), ("O", 1, 1, -1), ("O", 1, 1, 1), ("O", 1, 0, 1), ("P", 0, 0, 0),
+    ("A", 0, 1, 2, 1), ("A", 0, 1, 2, -1), ("A", 1, 0, 0, -1), ("A", 0, 0, 2, 1), ("P", 0, 1, 0), ("A", 1, 0, 0, 1),
+    ("A", 1, 1, 0, -1), ("A", 1, 1, 0, 1), ("A", 0, 0, 2, -1), ("N", 1, 0, -1), ("N", 1, 1, -1), ("A", 1, 0, 1, -1),
+    ("A", 1, 1, 3, -1), ("N", 1, 0, 1), ("A", 1, 1, 1, -1), ("A", 1, 1, 3, 1), ("A", 1, 0, 3, -1), ("N", 1, 1, 1),
+    ("A", 1, 0, 1, 1), ("P", 0, 0, 1), ("A", 1, 0, 3, 1), ("P", 0, 1, 2), ("P", 0, 0, 3), ("P", 0, 1, 1),
+    ("A", 1, 0, 2, 1), ("A", 1, 1, 2, 1), ("P", 0, 1, 3), ("P", 1, 0, 0), ("A", 1, 1, 2, -1), ("A", 1, 1, 1, 1),
+    ("P", 0, 0, 2), ("A", 1, 0, 2, -1), ("P", 1, 1, 0), ("P", 1, 1, 3), ("P", 1, 1, 1), ("P", 1, 0, 3), ("P", 1, 0, 1),
+    ("P", 1, 0, 2), ("P", 1, 1, 2),
+)
 
 
 def split(v):
@@ -119,8 +145,25 @@
 
     barrier = pltpu.get_barrier_semaphore()
     peers = [pair] + [go(o) for go in (at_z, at_y, at_x) for o in (1, -1)]
+    peers += [at_z(o) | pair for o in (1, -1)]
     for dev in peers:
         pl.semaphore_signal(barrier, inc=1, device_id=dev, device_id_type=MESH)
+
+    pl.semaphore_wait(barrier, len(peers))
+
+    for c in l_rg:
+        c.wait()
+    zin = {}
+
+    def zsend(s_from, s_to):
+        dev = at_z(1 if s_to in (2, 4, 6) else -1)
+        for n in range(2):
+            zin[s_to, n] = send(rg.at[s_from, core, n], rg.at[s_to, core, n], dev, "z", ("z", s_to, n))
+        send(rg.at[s_from, core], rg.at[s_to, core], dev | pair, "x", ("x", s_to))
+
+    zsend(0, 1)
+    zsend(0, 2)
+    send(rg.at[0, core], rg.at[0, core], pair, "p", ("x", 0))
 
     diag = lax.broadcasted_iota(jnp.int32, (BR, BR), 0) == lax.broadcasted_iota(jnp.int32, (BR, BR), 1)
     lane = lax.broadcasted_iota(jnp.int32, (BR, 128), 1)
@@ -142,22 +185,14 @@
             w2h[rows, n * WF : (n + 1) * WF] = hi
             w2l[rows, n * WF : (n + 1) * WF] = lo
 
-    pl.semaphore_wait(barrier, len(peers))
-
-    for c in l_rg:
-        c.wait()
-    zin, pr = {}, {}
-
-    def zsend(s_from, s_to):
-        o = 1 if s_to in (2, 4, 6) else -1
-        zin[s_to] = send(rg.at[s_from, core], rg.at[s_to, core], at_z(o), "z", ("z", s_to))
-
-    def psend(s):
-        pr[s] = send(rg.at[s, core], rg.at[s, core], pair, "pair", ("pair", s))
-
-    zsend(0, 1)
-    zsend(0, 2)
-    psend(0)
+    def rows_pass(*slots):
+        for s in slots:
+            for n in range(2):
+                zin[s, n].wait_recv()
+            if s < 6:
+                zsend(s, s + 2)
+
+    rows_pass(1, 2)
     for c in l_wd:
         c.wait()
 
@@ -168,21 +203,15 @@
         wdh[rows, :] = hi
         wdl[rows, :] = lo
 
-    def rows_pass(*slots):
-        for s in slots:
-            zin[s].wait_recv()
-            if s < 6:
-                zsend(s, s + 2)
-            psend(s)
-
-    rows_pass(1, 2, 3)
-
-    @pl.loop(0, WD // 64)
-    def _(i):
-        rows = pl.ds(pl.multiple_of(i * 64, 64), 64)
-        hi, lo = split(wof[rows, :])
-        woh[rows, :] = hi
-        wol[rows, :] = lo
+    rows_pass(3)
+
+    def split_out():
+        @pl.loop(0, WD // 64)
+        def _(i):
+            rows = pl.ds(pl.multiple_of(i * 64, 64), 64)
+            hi, lo = split(wof[rows, :])
+            woh[rows, :] = hi
+            wol[rows, :] = lo
 
     def project(k):
         both = rg[4 * k : 4 * k + 4]
@@ -219,57 +248,50 @@
 
     m1, m2 = {}, {}
 
-    def rs1_send(k):
-        for r in (2, 1, 0, 3):
-            for h in range(2):
-                go, av, _, _ = axes[h]
-                m1[k, h, r] = send(
-                    part.at[at_piece(k, h, r, wrap(av, 2))], r1.at[k, h, r], go(VIA[r]), "rs1r", ("r", k, h, r)
+    seen = set()
+
+    def once(key, wait):
+        if key not in seen:
+            seen.add(key)
+            wait()
+
+    def relay_send(k, h, r):
+        go, av, _, _ = axes[h]
+        m1[k, h, r] = send(
+            part.at[at_piece(k, h, r, wrap(av, 2))], r1.at[k, h, r], go(VIA[r]), "rs1r", ("r", k, h, r)
+        )
+
+    def direct_send(k, h, r):
+        go, av, _, _ = axes[h]
+        send(part.at[at_piece(k, h, r, wrap(av, -VIA[r]))], c1.at[k, h, r, 1], go(-VIA[r]), "rs1d", ("c", k, h, r))
+
+    def relay_add(k, h, r):
+        go, av, _, _ = axes[h]
+        m1[k, h, r].wait_recv()
+        r1[k, h, r] = r1[k, h, r] + part[at_piece(k, h, r, wrap(av, VIA[r]))]
+        send(r1.at[k, h, r], c1.at[k, h, r, 0], go(VIA[r]), "rs1c", ("c", k, h, r))
+
+    def first_sum(k, h, r):
+        _, av, go, _ = axes[h]
+        arrived(("c", k, h, r), c1.at[k, h, r])
+        q1[k, h, r] = part[at_piece(k, h, r, av)] + c1[k, h, r, 0] + c1[k, h, r, 1]
+        if r == 2:
+            for d, cols in ((1, LO), (-1, HI)):
+                n = (1 - d) // 2
+                m2[k, h, d] = send(
+                    q1.at[k, h, 2, :, cols], r2.at[k, h, n, :, cols], go(d), "rs2", ("r2", k, h, d)
                 )
-
-    def rs1_direct(k):
-        for r in (2, 1, 3, 0):
-            for h in range(2):
-                go, av, _, _ = axes[h]
-                send(
-                    part.at[at_piece(k, h, r, wrap(av, -VIA[r]))], c1.at[k, h, r, 1], go(-VIA[r]), "rs1d", ("c", k, h, r)
-                )
-
-    def rs1_relay(k):
-        for r in (2, 1, 0, 3):
-            for h in range(2):
-                go, av, _, _ = axes[h]
-                m1[k, h, r].wait_recv()
-                r1[k, h, r] = r1[k, h, r] + part[at_piece(k, h, r, wrap(av, VIA[r]))]
-                send(r1.at[k, h, r], c1.at[k, h, r, 0], go(VIA[r]), "rs1c", ("c", k, h, r))
-
-    def rs1_final(k):
-        for r in (2, 1, 3, 0):
-            for h in range(2):
-                _, av, go, _ = axes[h]
-                arrived(("c", k, h, r), c1.at[k, h, r])
-                q1[k, h, r] = part[at_piece(k, h, r, av)] + c1[k, h, r, 0] + c1[k, h, r, 1]
-                if r == 2:
-                    m2[k, h, 1] = send(
-                        q1.at[k, h, 2, :, LO], r2.at[k, h, 0, :, LO], go(1), "rs2", ("rp", k, h)
-                    )
-                    m2[k, h, -1] = send(
-                        q1.at[k, h, 2, :, HI], r2.at[k, h, 1, :, HI], go(-1), "rs2", ("rm", k, h)
-                    )
-                elif r == 1:
-                    send(q1.at[k, h, 1, :, HI], c2.at[k, h, 0, :, HI], go(1), "rs2", ("c2", k, h))
-                elif r == 3:
-                    send(q1.at[k, h, 3, :, LO], c2.at[k, h, 1, :, LO], go(-1), "rs2", ("c2", k, h))
-
-    def rs2_relay(k):
-        for h in range(2):
-            _, _, go, _ = axes[h]
-            m2[k, h, 1].wait_recv()
-            r2[k, h, 0, :, LO] = r2[k, h, 0, :, LO] + q1[k, h, 1, :, LO]
-            send(r2.at[k, h, 0, :, LO], c2.at[k, h, 0, :, LO], go(1), "rs2", ("c2", k, h))
-            m2[k, h, -1].wait_recv()
-            r2[k, h, 1, :, HI] = r2[k, h, 1, :, HI] + q1[k, h, 3, :, HI]
-            send(r2.at[k, h, 1, :, HI], c2.at[k, h, 1, :, HI], go(-1), "rs2", ("c2", k, h))
+        elif r == 1:
+            send(q1.at[k, h, 1, :, HI], c2.at[k, h, 0, :, HI], go(1), "rs2", ("c2", k, h))
+        elif r == 3:
+            send(q1.at[k, h, 3, :, LO], c2.at[k, h, 1, :, LO], go(-1), "rs2", ("c2", k, h))
+
+    def second_add(k, h, d):
+        _, _, go, _ = axes[h]
+        n, r, cols = (0, 1, LO) if d == 1 else (1, 3, HI)
+        m2[k, h, d].wait_recv()
+        r2[k, h, n, :, cols] = r2[k, h, n, :, cols] + q1[k, h, r, :, cols]
+        send(r2.at[k, h, n, :, cols], c2.at[k, h, n, :, cols], go(d), "rs2", ("c2", k, h))
 
     def gate(k):
         sums = []
@@ -304,41 +326,33 @@
 
     g1, g2 = {}, {}
 
-    def ag_across(k, h, r):
+    def near(k, h, d):
+        once(("b", k, h, d), g1[k, h, d].wait_recv)
+
+    def across(k, h, r, d):
         go, av, _, _ = axes[h]
-        for d in (1, -1):
-            into = ("a", k, h, r) if d == VIA[r] else ("done", k)
-            g2[k, h, r, d] = fsend(k, h, r, av, go(d), ("a", k), into)
-
-    def ag_own(k):
-        for h in range(2):
-            _, av, go, _ = axes[h]
-            for d in (1, -1):
-                g1[k, h, d] = fsend(k, h, 0, av, go(d), "ag1", ("b", k, h, d))
-        for h in range(2):
-            ag_across(k, h, 0)
-
-    def ag_near(k):
-        for h in range(2):
-            _, av, go, _ = axes[h]
-            g1[k, h, 1].wait_recv()
-            fsend(k, h, 3, av, go(1), "ag1", ("b2", k, h), LO)
-            g1[k, h, -1].wait_recv()
-            fsend(k, h, 1, av, go(-1), "ag1", ("b2", k, h), HI)
-        for r in (3, 1):
-            for h in range(2):
-                ag_across(k, h, r)
-
-    def ag_far(k):
-        for h in range(2):
-            arrived(("b2", k, h), q1.at[k, h, 0])
-            ag_across(k, h, 2)
-
-    def ag_pass(k, r):
-        for h in range(2):
-            go, av, _, _ = axes[h]
-            g2[k, h, r, VIA[r]].wait_recv()
-            fsend(k, h, r, wrap(av, -VIA[r]), go(VIA[r]), "pass", ("done", k))
+        if r == 3:
+            near(k, h, 1)
+        elif r == 1:
+            near(k, h, -1)
+        elif r == 2:
+            once(("b2", k, h), lambda: arrived(("b2", k, h), q1.at[k, h, 0]))
+        into = ("a", k, h, r) if d == VIA[r] else ("done", k)
+        g2[k, h, r, d] = fsend(k, h, r, av, go(d), ("a", k), into)
+
+    def own_send(k, h, d):
+        _, av, go, _ = axes[h]
+        g1[k, h, d] = fsend(k, h, 0, av, go(d), "ag1", ("b", k, h, d))
+
+    def near_pass(k, h, d):
+        _, av, go, _ = axes[h]
+        near(k, h, d)
+        fsend(k, h, 3 if d == 1 else 1, av, go(d), "ag1", ("b2", k, h), LO if d == 1 else HI)
+
+    def across_pass(k, h, r):
+        go, av, _, _ = axes[h]
+        g2[k, h, r, VIA[r]].wait_recv()
+        fsend(k, h, r, wrap(av, -VIA[r]), go(VIA[r]), "pass", ("done", k))
 
     def ag_done(k):
         arrived(("done", k), full.at[k, :, :, :, cs[0]])
@@ -354,13 +368,16 @@
         resid = rg[4 * k : 4 * k + 4, :, 0].reshape(128, WD)
         t = dn * gain[...] * inv - resid * coef
         tpart[k] = t.reshape(4, 2, BR, WD)
-        pf[k] = send(tpart.at[k, :, other], tpair.at[k], pair, "pf", ("pf", k))
+        for n in (3, 2, 1, 0):
+            pf[k, n] = send(tpart.at[k, n, other], tpair.at[k, n], pair, "pf", ("pf", k, n))
 
     def input_grad_send(k):
-        pf[k].wait_recv()
-        usum[k] = tpart[k, :, core] + tpair[k]
-        for s in range(4 * k + 3, max(4 * k, 1) - 1, -1):
-            send(usum.at[k, s % 4], rz.at[s], at_z(OFF[s]), "zf", "zf")
+        for n in (3, 2, 1, 0):
+            pf[k, n].wait_recv()
+            usum[k, n] = tpart[k, n, core] + tpair[k, n]
+            s = 4 * k + n
+            if s:
+                send(usum.at[k, n], rz.at[s], at_z(OFF[s]), "zf", "zf")
 
     def weight_grads():
         inv = full[:, :, :, :, 2688:].reshape(ROWS, 128)[:, 0:1]
@@ -416,7 +433,7 @@
 
     def rows_pair(k):
         for s in range(4 * k, 4 * k + 4):
-            pr[s].wait_recv()
+            arrived(("x", s), rg.at[s, 0])
 
     outs = []
 
@@ -440,27 +457,35 @@
         gres[wide] = total
         for s in range(7, 0, -1):
             gz[s] = send(gres.at[wide], gres.at[wide], at_z(OFF[s]), "g", ("g", s))
-        send(gres.at[wide], gres.at[wide], pair, "g", "gp")
+        send(gres.at[wide], gres.at[wide], pair, "g", ("gp", 0))
         outs.append(local(gres.at[wide], gres_o))
 
-    def resid_all():
-        for s in range(1, 8):
+    def resid_from(s):
+        return lax.rem(z + (NZ - OFF[s]), NZ)
+
+    def resid_pass(g):
+        for s in range(max(4 * g, 1), 4 * g + 4):
             gz[s].wait_recv()
-            w = 2 * lax.rem(z + (NZ - OFF[s]), NZ) + core
-            send(gres.at[w], gres.at[w], pair, "g", "gp")
-
-    def resid_pair():
-        arrived("gp", gres.at[0:8])
-
-    def d_attn_part():
-        gh, gl = split(gres[...].reshape(ROWS, WD))
+            w = 2 * resid_from(s) + core
+            send(gres.at[w], gres.at[w], pair, "g", ("gp", g))
+        arrived(("gp", g), gres.at[0:4])
+
+    def d_attn_part(g):
+        blocks = [2 * resid_from(s) + p for s in range(4 * g, 4 * g + 4) for p in range(2)]
+        gh, gl = split(jnp.concatenate([gres[w] for w in blocks], axis=0))
         gg = jnp.concatenate([gh, gl], axis=0)
         for h in range(2):
             cols = slice(h * HD, (h + 1) * HD)
             two = nt(gg, woh[cols, :])
-            da[h] = (two[:ROWS] + two[ROWS:] + nt(gh, wol[cols, :])).reshape(16, BR, HD)
-            for n, o in enumerate(ctx_offsets):
-                send(da.at[h, ctx_of(*o)], rda.at[h, n], at_ctx(*o), "di", ("di", h))
+            out = two[:128] + two[128:] + nt(gh, wol[cols, :])
+            for n, w in enumerate(blocks):
+                da[h, w] = out[n * BR : (n + 1) * BR]
+            for w in blocks:
+
+                @pl.when(w != me)
+                def _(w=w):
+                    dev = {"y": w // NX, "x": lax.rem(w, NX)}
+                    send(da.at[h, w], rda.at[h, me], dev, "di", ("di", h))
 
     def out_grad():
         oh, ol = split(qol[:, :, 256:512].reshape(ROWS, WD).T)
@@ -470,16 +495,16 @@
         outs.append(local(gwo, gwo_o))
 
     def d_attn_sum(h):
-        arrived(("di", h), rda.at[h])
+        arrived(("di", h), rda.at[h, 0:15])
         own = da[h, me]
-        for n in range(NCTX - 1):
-            own = own + rda[h, n]
+        for o in ctx_offsets:
+            own = own + rda[h, ctx_of(*o)]
         dat[h, me] = own
         for o in ctx_offsets:
             send(dat.at[h, me], dat.at[h, me], at_ctx(*o), "do", ("do", h))
 
     def d_attn_all(h):
-        arrived(("do", h), rda.at[h])
+        arrived(("do", h), rda.at[h, 0:15])
 
     def query_grad(h):
         d_attn = dat[h].reshape(ROWS, HD)
@@ -520,48 +545,28 @@
         outs.append(local(gqs, gq_o))
         sixteen = full.at[0, :, :, :, cs[0]]
         for out, like in (
-            ("z", rg.at[1:8, 0]), ("pair", rg.at[:, 0]), ("kv", kv.at[:, 0]), ("qo", qol.at[0:15]),
+            ("z", rg.at[1:8, 0]), ("x", rg.at[1:8, 0]), ("p", rg.at[0, 0]), ("kv", kv.at[:, 0]), ("qo", qol.at[0:15]),
             ("rs1r", sixteen), ("rs1d", sixteen), ("rs1c", sixteen), ("rs2", q1.at[:, :, 0:3]),
             ("ag1", q1.at[:, :, 0:3]), (("a", 0), sixteen), (("a", 1), sixteen), ("pass", sixteen),
-            ("pf", tpair), ("zf", rz.at[1:8]), ("g", gres.at[0:15]), ("di", rda), ("do", rda), ("qi", rdq),
+            ("pf", tpair), ("zf", rz.at[1:8]), ("g", gres.at[0:15]), ("di", rda.at[:, 0:15]), ("do", rda.at[:, 0:15]), ("qi", rdq),
         ):
             gone(out, like)
         for c in outs:
             c.wait()
 
-    rows_pair(0)
-    project(0)
-    rs1_send(0)
-    rs1_direct(0)
-    rows_pass(4, 5, 6)
-    rs1_relay(0)
-    rows_pass(7)
-    rows_pair(1)
-    project(1)
-    rs1_send(1)
-    rs1_final(0)
-    rs1_direct(1)
-    start_kv()
-    rs2_relay(0)
-    rs1_relay(1)
-    gate(0)
-    ag_own(0)
-    rs1_final(1)
-    ag_near(0)
-    ag_pass(0, 0)
-    rs2_relay(1)
-    ag_far(0)
-    gate(1)
-    ag_own(1)
-    ag_pass(0, 3)
-    ag_pass(0, 1)
-    ag_near(1)
-    ag_pass(0, 2)
-    ag_pass(1, 0)
-    ag_far(1)
-    ag_pass(1, 3)
-    ag_pass(1, 1)
-    ag_pass(1, 2)
+    def enter(k):
+        rows_pair(k)
+        project(k)
+        if k == 1:
+            start_kv()
+
+    steps = {
+        "S": relay_send, "D": direct_send, "R": relay_add, "F": first_sum, "T": second_add, "G": gate,
+        "O": own_send, "A": across, "N": near_pass, "P": across_pass, "Z": rows_pass, "J": enter,
+    }
+    enter(0)
+    for step in ORDER:
+        steps[step[0]](*step[1:])
     input_grad(0)
     input_grad_send(0)
     input_grad(1)
@@ -570,10 +575,12 @@
     weight_grads()
     store_weights()
     attention_split()
+    split_out()
     resid_own()
-    resid_all()
-    resid_pair()
-    d_attn_part()
+    resid_pass(0)
+    d_attn_part(0)
+    resid_pass(1)
+    d_attn_part(1)
     qo_wait()
     out_grad()
     attention_probs(0)
@@ -622,14 +629,14 @@
         V((2, 4, 4, 8, WIDTH), F32),
         V((2, 4, 2, BR, WD), F32), V((2, 4, BR, WD), F32), V((2, 4, BR, WD), F32),
         V((8, BR, WD), F32),
-        V((16, BR, WD), F32), V((2, 16, BR, HD), F32), V((2, 15, BR, HD), F32), V((2, 16, BR, HD), F32),
+        V((16, BR, WD), F32), V((2, 16, BR, HD), F32), V((2, 16, BR, HD), F32), V((2, 16, BR, HD), F32),
         V((2, ROWS, 2 * KEYS), F32),
         V((2 * ROWS, 2 * HD), F32),
         V((2, 16, BR, HD), F32), V((2, 15, BR, HD), F32),
         V((WD, 2 * WF), F32), V((WF, WD), F32), V((WD, WD), F32), V((BR, WD), F32),
         pltpu.SemaphoreType.DMA((18,)),
-        pltpu.SemaphoreType.DMA((18,)),
-        pltpu.SemaphoreType.DMA((108,)),
+        pltpu.SemaphoreType.DMA((19,)),
+        pltpu.SemaphoreType.DMA((NSEM,)),
     ]
     hbm = pl.BlockSpec(memory_space=pltpu.HBM)
     anyspec = pl.BlockSpec(memory_space=pl.ANY)

time: 91 us -> 88.3 us (0.970)
  Pallas kernels: 90.3 us -> 87.6 us
    pallas_call x1, Pallas kernels: 88.6 us -> 85.9 us  [shards(): pl.pallas_call(kernel, out_shape=(shape((WD, WF), F32), shape((WD, WF), F...]
where the time goes in v3:
time: 88.3 us; the launch traced here: 88.2 us
  Pallas kernels  87.6 us (99%)
    pallas_call x1, Pallas kernels, shards(): pl.pallas_call(kernel, out_shape=(shape((WD, WF), F32), shape((WD, WF), F...  85.9 us

profile of v3, /device:TPU:1, one launch (start us, length us, event | category | flops | bytes accessed | tf_op | source)
XLA Modules:
  0.0 88.2 jit_solution(3718009685416839798)
XLA Ops:
  0.6 85.9 %shard_map.163 = (f32[256,896]{1,0:T(8,128)S(1)}, f32[256,896]{1,0:T(8,128)S(1)}, f32[896,256]{1,0:T(8,128)S(1)}, f32[256,256]{1,0:T(8,128)S(1)}, f32[16,256]{1,0:T(8,128)S(1)}, /*index=5*/f32[16,256]{1,0:T(8,128)S(1)}) custom-call(f32[16,256]{1,0:T(8,128)} %resid_h.1, f32[16,256]{1,0:T(8,128)} %grad_h.1, f32[1,256]{1,0:T(1,128)} %bitcast.1, ...), custom_call_target="tpu_custom_call" | custom-call | tf_op jit(solution)/shard_map/pallas_call | solution.py:643
  86.6 1.7 %shard_map.164 = (f32[256,896]{1,0:T(8,128)}, f32[256,896]{1,0:T(8,128)}, f32[896,256]{1,0:T(8,128)}, f32[256,256]{1,0:T(8,128)}, f32[16,256]{1,0:T(8,128)}, /*index=5*/f32[16,256]{1,0:T(8,128)}) custom-call(f32[256,896]{1,0:T(8,128)S(1)} %get-tuple-element.12.refs_0_, f32[256,896]{1,0:T(8,128)S(1)} %get-tuple-element.13.refs_1_, ...), custom_call_target="tpu_custom_call" | custom-call | tf_op jit(solution)/shard_map/pallas_call | solution.py:656

commit v4 on v3

--- a/solution.py
+++ b/solution.py
@@ -22,7 +22,7 @@
 HALF = 11 * 128
 WIDTH = 2 * HALF
 KEYS = 1024
-NSEM = 122
+NSEM = 109
 LIMIT = 48 * 1024 * 1024
 CONTEXT = 32768
 SCALE = 1.0 / math.sqrt(HD)
@@ -157,9 +157,8 @@
 
     def zsend(s_from, s_to):
         dev = at_z(1 if s_to in (2, 4, 6) else -1)
-        for n in range(2):
-            zin[s_to, n] = send(rg.at[s_from, core, n], rg.at[s_to, core, n], dev, "z", ("z", s_to, n))
-        send(rg.at[s_from, core], rg.at[s_to, core], dev | pair, "x", ("x", s_to))
+        zin[s_to] = send(rg.at[s_from, core], rg.at[s_to, core], dev, "z", ("z", s_to))
+        send(rg.at[s_from, core], rg.at[s_to, core], dev | pair, "x", ("x", s_to // 4))
 
     zsend(0, 1)
     zsend(0, 2)
@@ -187,8 +186,7 @@
 
     def rows_pass(*slots):
         for s in slots:
-            for n in range(2):
-                zin[s, n].wait_recv()
+            zin[s].wait_recv()
             if s < 6:
                 zsend(s, s + 2)
 
@@ -432,8 +430,7 @@
             probs[h, :, keys] = jnp.where(pos <= row, jnp.exp(s - lse), 0.0)
 
     def rows_pair(k):
-        for s in range(4 * k, 4 * k + 4):
-            arrived(("x", s), rg.at[s, 0])
+        arrived(("x", k), rg.at[0:4, 0])
 
     outs = []
 

time: 88.3 us -> 88.1 us (level)
  no operation moved by 1% of the time
where the time goes in v4:
time: 88.1 us; the launch traced here: 88 us
  Pallas kernels  87.4 us (99%)
    pallas_call x1, Pallas kernels, shards(): pl.pallas_call(kernel, out_shape=(shape((WD, WF), F32), shape((WD, WF), F...  85.7 us

profile of v4, /device:TPU:1, one launch (start us, length us, event | category | flops | bytes accessed | tf_op | source)
XLA Modules:
  0.0 88.0 jit_solution(6414193338049303973)
XLA Ops:
  0.6 85.7 %shard_map.163 = (f32[256,896]{1,0:T(8,128)S(1)}, f32[256,896]{1,0:T(8,128)S(1)}, f32[896,256]{1,0:T(8,128)S(1)}, f32[256,256]{1,0:T(8,128)S(1)}, f32[16,256]{1,0:T(8,128)S(1)}, /*index=5*/f32[16,256]{1,0:T(8,128)S(1)}) custom-call(f32[16,256]{1,0:T(8,128)} %resid_h.1, f32[16,256]{1,0:T(8,128)} %grad_h.1, f32[1,256]{1,0:T(1,128)} %bitcast.1, ...), custom_call_target="tpu_custom_call" | custom-call | tf_op jit(solution)/shard_map/pallas_call | solution.py:640
  86.4 1.7 %shard_map.164 = (f32[256,896]{1,0:T(8,128)}, f32[256,896]{1,0:T(8,128)}, f32[896,256]{1,0:T(8,128)}, f32[256,256]{1,0:T(8,128)}, f32[16,256]{1,0:T(8,128)}, /*index=5*/f32[16,256]{1,0:T(8,128)}) custom-call(f32[256,896]{1,0:T(8,128)S(1)} %get-tuple-element.12.refs_0_, f32[256,896]{1,0:T(8,128)S(1)} %get-tuple-element.13.refs_1_, ...), custom_call_target="tpu_custom_call" | custom-call | tf_op jit(solution)/shard_map/pallas_call | solution.py:653
